TPU v7x, 32 devices: a whole 2x2x4 slice. The times are simulated.
32 devices in a mesh: dp: 8 (over y, x, core), mp: 4 (over z).
Axes of the slice: x: 2, y: 2, z: 4, core: 2. Of those that a mesh axis runs over, the one named last changes fastest.
Arguments:
- activations: bfloat16 [128, 288, 768], P(('dp', 'mp')), may hold values from -2.5 to 2.5
- cotangent: bfloat16 [128, 288, 768], P(('dp', 'mp')), may hold values from -2.5 to 2.5
- segments: int32 [128, 288], P('dp'), may hold values from 0 to 2, never falling along the last dimension, each value on 1 to 160 neighbouring positions
- triple_weight: bfloat16 [3, 768, 768], P(None, None, 'mp'), may hold values from -0.21875 to 0.21875
- query_value_bias: bfloat16 [2, 12, 64], P(None, 'mp'), may hold values from -1.5 to 1.5
- output_weight: bfloat16 [768, 768], P('mp'), may hold values from -0.875 to 0.875
- expand_weight: bfloat16 [768, 3072], P(None, 'mp'), may hold values from -0.21875 to 0.21875
- expand_bias: bfloat16 [48, 64], P('mp'), may hold values from -1.5 to 1.5
- shrink_weight: bfloat16 [3072, 768], P('mp'), may hold values from -0.109375 to 0.109375
- vector_params: bfloat16 [6, 768], replicated
- triple_master: float32 [3, 768, 768], P(None, 'dp', 'mp'), may hold values from -0.21875 to 0.21875
- triple_first: float32 [3, 768, 768], P(None, 'dp', 'mp'), may hold values from -144 to 144
- triple_second: float32 [3, 768, 768], P(None, 'dp', 'mp'), may hold values from 2211.84 to 8847.36
- query_value_master: float32 [2, 12, 64], P(None, 'mp', 'dp'), may hold values from -1.5 to 1.5
- query_value_first: float32 [2, 12, 64], P(None, 'mp', 'dp'), may hold values from -192 to 192
- query_value_second: float32 [2, 12, 64], P(None, 'mp', 'dp'), may hold values from 3944.448 to 15851.52
- output_master: float32 [768, 768], P('mp', 'dp'), may hold values from -0.875 to 0.875
- output_first: float32 [768, 768], P('mp', 'dp'), may hold values from -57.6 to 57.6
- output_second: float32 [768, 768], P('mp', 'dp'), may hold values from 353.8944 to 1400.832
- expand_master: float32 [768, 3072], P('dp', 'mp'), may hold values from -0.21875 to 0.21875
- expand_first: float32 [768, 3072], P('dp', 'mp'), may hold values from -96 to 96
- expand_second: float32 [768, 3072], P('dp', 'mp'), may hold values from 995.328 to 3944.448
- expand_bias_master: float32 [48, 64], P('mp', 'dp'), may hold values from -1.5 to 1.5
- expand_bias_first: float32 [48, 64], P('mp', 'dp'), may hold values from -96 to 96
- expand_bias_second: float32 [48, 64], P('mp', 'dp'), may hold values from 995.328 to 3944.448
- shrink_master: float32 [3072, 768], P('mp', 'dp'), may hold values from -0.109375 to 0.109375
- shrink_first: float32 [3072, 768], P('mp', 'dp'), may hold values from -192 to 192
- shrink_second: float32 [3072, 768], P('mp', 'dp'), may hold values from 3944.448 to 15851.52
- vector_master: float32 [6, 768], P(None, ('dp', 'mp'))
- vector_first: float32 [6, 768], P(None, ('dp', 'mp')), may hold values from -384 to 384
- vector_second: float32 [6, 768], P(None, ('dp', 'mp')), may hold values from 15851.52 to 62668.8
Outputs:
- block_output: bfloat16 [128, 288, 768], P(('dp', 'mp'))
- input_grad: float32 [128, 288, 768], P(('dp', 'mp'))
- triple_master_new: float32 [3, 768, 768], P(None, 'dp', 'mp')
- triple_first_new: float32 [3, 768, 768], P(None, 'dp', 'mp')
- triple_second_new: float32 [3, 768, 768], P(None, 'dp', 'mp')
- triple_copy: bfloat16 [3, 768, 768], P(None, 'dp', 'mp')
- query_value_master_new: float32 [2, 12, 64], P(None, 'mp', 'dp')
- query_value_first_new: float32 [2, 12, 64], P(None, 'mp', 'dp')
- query_value_second_new: float32 [2, 12, 64], P(None, 'mp', 'dp')
- query_value_copy: bfloat16 [2, 12, 64], P(None, 'mp', 'dp')
- output_master_new: float32 [768, 768], P('mp', 'dp')
- output_first_new: float32 [768, 768], P('mp', 'dp')
- output_second_new: float32 [768, 768], P('mp', 'dp')
- output_copy: bfloat16 [768, 768], P('mp', 'dp')
- expand_master_new: float32 [768, 3072], P('dp', 'mp')
- expand_first_new: float32 [768, 3072], P('dp', 'mp')
- expand_second_new: float32 [768, 3072], P('dp', 'mp')
- expand_copy: bfloat16 [768, 3072], P('dp', 'mp')
- expand_bias_master_new: float32 [48, 64], P('mp', 'dp')
- expand_bias_first_new: float32 [48, 64], P('mp', 'dp')
- expand_bias_second_new: float32 [48, 64], P('mp', 'dp')
- expand_bias_copy: bfloat16 [48, 64], P('mp', 'dp')
- shrink_master_new: float32 [3072, 768], P('mp', 'dp')
- shrink_first_new: float32 [3072, 768], P('mp', 'dp')
- shrink_second_new: float32 [3072, 768], P('mp', 'dp')
- shrink_copy: bfloat16 [3072, 768], P('mp', 'dp')
- vector_master_new: float32 [6, 768], P(None, ('dp', 'mp'))
- vector_first_new: float32 [6, 768], P(None, ('dp', 'mp'))
- vector_second_new: float32 [6, 768], P(None, ('dp', 'mp'))
- vector_copy: bfloat16 [6, 768], P(None, ('dp', 'mp'))
Inputs may be any that keep to these rules, and one draw needn't show every extreme that they name: `segments`: along a row the pair numbers never fall; each pair has 1 to 160 tokens, and each row has one pair of exactly 160.
All inputs are finite; a program needn't handle non-finite values.
Results may differ from a plain program's by a relative error of at most 0.018.
Values may be sent and summed in bfloat16 or wider, within the bound.
A program may use at most 256 MiB of HBM per device.

v0:
```python
import jax
import jax.numpy as jnp
from jax import lax
from jax.sharding import PartitionSpec as P

D = 768
HEAD = 64
FF = 3072
MB = 4
STEP = 10


NORM_EPS = 1e-05
BETA_ONE = 0.5
BETA_TWO = 0.6
ADAM_EPS = 1e-08
WEIGHT_DECAY = 0.01
MASKED = -1e30
SQRT_HALF = 0.7071067811865476
INV_ROOT_TAU = 0.3989422804014327


def norm_forward(summed, gain, shift):
    centre = summed - jnp.mean(summed, axis=-1, keepdims=True)
    scale = lax.rsqrt(jnp.mean(centre * centre, axis=-1, keepdims=True) + NORM_EPS)
    normed = centre * scale
    return (gain * normed + shift, normed, scale)


def norm_backward(gradient, gain, normed, scale):
    scaled = gradient * gain
    centred = scaled - jnp.mean(scaled, axis=-1, keepdims=True)
    return scale * (centred - normed * jnp.mean(scaled * normed, axis=-1, keepdims=True))


def gelu(inputs):
    return 0.5 * inputs * (1.0 + jax.scipy.special.erf(inputs * SQRT_HALF))


def gelu_slope(inputs):
    cumulative = 0.5 * (1.0 + jax.scipy.special.erf(inputs * SQRT_HALF))
    return cumulative + inputs * jnp.exp(-0.5 * inputs * inputs) * INV_ROOT_TAU


def attention_scores(projected, allowed, head_count):
    row_count, length = (projected.shape[0], projected.shape[1])
    parted = projected.reshape(row_count, length, 3, head_count, HEAD)
    queries = parted[:, :, 0]
    key_rows = parted[:, :, 1]
    values = parted[:, :, 2]
    scores = jnp.einsum(
        "rqhc,rkhc->rhqk", queries, key_rows, preferred_element_type=jnp.float32
    ) * HEAD ** (-0.5)
    return (jnp.where(allowed[:, None], scores, MASKED), queries, key_rows, values)


def attend(projected, allowed, head_count):
    row_count, length = (projected.shape[0], projected.shape[1])
    scores, queries, key_rows, values = attention_scores(projected, allowed, head_count)
    row_max = jnp.max(scores, axis=-1, keepdims=True)
    weights = jnp.exp(scores - row_max)
    row_total = jnp.sum(weights, axis=-1, keepdims=True)
    probabilities = (weights / row_total).astype(jnp.bfloat16)
    context = jnp.einsum(
        "rhqk,rkhc->rqhc", probabilities, values, preferred_element_type=jnp.float32
    )
    context = context.astype(jnp.bfloat16).reshape(row_count, length, head_count * HEAD)
    return (context, row_max + jnp.log(row_total))


def attend_back(projected, allowed, log_total, dcontext, head_count):
    row_count, length = (projected.shape[0], projected.shape[1])
    scores, queries, key_rows, values = attention_scores(projected, allowed, head_count)
    probabilities = jnp.exp(scores - log_total)
    grad_context = dcontext.reshape(row_count, length, head_count, HEAD)
    grad_values = jnp.einsum(
        "rhqk,rqhc->rkhc",
        probabilities.astype(jnp.bfloat16),
        grad_context,
        preferred_element_type=jnp.float32,
    )
    grad_probs = jnp.einsum(
        "rqhc,rkhc->rhqk", grad_context, values, preferred_element_type=jnp.float32
    )
    row_inner = jnp.sum(probabilities * grad_probs, axis=-1, keepdims=True)
    grad_scores = (probabilities * (grad_probs - row_inner)).astype(jnp.bfloat16)
    grad_queries = jnp.einsum(
        "rhqk,rkhc->rqhc", grad_scores, key_rows, preferred_element_type=jnp.float32
    ) * HEAD ** (-0.5)
    grad_keys = jnp.einsum(
        "rhqk,rqhc->rkhc", grad_scores, queries, preferred_element_type=jnp.float32
    ) * HEAD ** (-0.5)
    stacked = jnp.stack([grad_queries, grad_keys, grad_values], axis=2)
    return stacked.astype(jnp.bfloat16).reshape(row_count, length, 3, head_count * HEAD)


def adam_update(master, first, second, gradient, rate):
    first_new = BETA_ONE * first + (1.0 - BETA_ONE) * gradient
    second_new = BETA_TWO * second + (1.0 - BETA_TWO) * gradient * gradient
    corrected = first_new / (1.0 - BETA_ONE**STEP)
    spread = jnp.sqrt(second_new / (1.0 - BETA_TWO**STEP))
    master_new = master - rate * (corrected / (spread + ADAM_EPS) + WEIGHT_DECAY * master)
    return (master_new, first_new, second_new, master_new.astype(jnp.bfloat16))


def per_device(
    activations,
    cotangent,
    segments,
    triple_weight,
    query_value_bias,
    output_weight,
    expand_weight,
    expand_bias,
    shrink_weight,
    vector_params,
    triple_master,
    triple_first,
    triple_second,
    query_value_master,
    query_value_first,
    query_value_second,
    output_master,
    output_first,
    output_second,
    expand_master,
    expand_first,
    expand_second,
    expand_bias_master,
    expand_bias_first,
    expand_bias_second,
    shrink_master,
    shrink_first,
    shrink_second,
    vector_master,
    vector_first,
    vector_second,
):
    group_count = lax.axis_size("mp")
    triple_local, query_value_local, output_local = (triple_weight, query_value_bias, output_weight)
    expand_local, expand_bias_local, shrink_local = (expand_weight, expand_bias, shrink_weight)
    gains = vector_params.astype(jnp.float32)
    head_count = triple_local.shape[2] // HEAD
    width = head_count * HEAD
    bias_pair = query_value_local.reshape(2, width).astype(jnp.float32)
    bias_add = jnp.stack([bias_pair[0], jnp.zeros_like(bias_pair[0]), bias_pair[1]])
    expand_shift = expand_bias_local.reshape(-1).astype(jnp.float32)
    micro_rows = activations.shape[0] // MB
    length = activations.shape[1]
    segment_blocks = segments.reshape(group_count, MB, micro_rows, length)
    triple_grad = jnp.zeros(triple_local.shape, jnp.float32)
    bias_grad = jnp.zeros((3, width), jnp.float32)
    output_grad = jnp.zeros(output_local.shape, jnp.float32)
    expand_grad = jnp.zeros(expand_local.shape, jnp.float32)
    expand_shift_grad = jnp.zeros(expand_shift.shape, jnp.float32)
    shrink_grad = jnp.zeros(shrink_local.shape, jnp.float32)
    vector_grad = jnp.zeros(gains.shape, jnp.float32)
    outputs = []
    input_grads = []
    for micro_index in range(MB):
        own_inputs = activations[micro_index * micro_rows : (micro_index + 1) * micro_rows]
        own_back = cotangent[micro_index * micro_rows : (micro_index + 1) * micro_rows].astype(
            jnp.float32
        )
        full_inputs = lax.all_gather(own_inputs, "mp", axis=0, tiled=True)
        seg_rows = segment_blocks[:, micro_index].reshape(-1, length)
        allowed = seg_rows[:, :, None] == seg_rows[:, None, :]
        projected = jnp.einsum(
            "rld,jde->rlje", full_inputs, triple_local, preferred_element_type=jnp.float32
        )
        projected = (projected + bias_add).astype(jnp.bfloat16)
        context, log_total = attend(projected, allowed, head_count)
        attended = lax.psum_scatter(
            jnp.einsum(
                "rle,ed->rld", context, output_local, preferred_element_type=jnp.float32
            ).astype(jnp.bfloat16),
            "mp",
            scatter_dimension=0,
            tiled=True,
        ).astype(jnp.float32)
        mixed = own_inputs.astype(jnp.float32) + attended + gains[2]
        hidden, normed_one, scale_one = norm_forward(mixed, gains[0], gains[1])
        hidden_low = hidden.astype(jnp.bfloat16)
        full_hidden = lax.all_gather(hidden_low, "mp", axis=0, tiled=True)
        expanded = (
            jnp.einsum("rld,df->rlf", full_hidden, expand_local, preferred_element_type=jnp.float32)
            + expand_shift
        )
        active = gelu(expanded).astype(jnp.bfloat16)
        shrunk = lax.psum_scatter(
            jnp.einsum(
                "rlf,fd->rld", active, shrink_local, preferred_element_type=jnp.float32
            ).astype(jnp.bfloat16),
            "mp",
            scatter_dimension=0,
            tiled=True,
        ).astype(jnp.float32)
        summed = hidden + shrunk + gains[5]
        result, normed_two, scale_two = norm_forward(summed, gains[3], gains[4])
        outputs.append(result.astype(jnp.bfloat16))
        dsummed = norm_backward(own_back, gains[3], normed_two, scale_two)
        dsummed_low = dsummed.astype(jnp.bfloat16)
        full_dsummed = lax.all_gather(dsummed_low, "mp", axis=0, tiled=True)
        dactive = jnp.einsum(
            "rld,fd->rlf", full_dsummed, shrink_local, preferred_element_type=jnp.float32
        )
        dexpanded = (dactive * gelu_slope(expanded)).astype(jnp.bfloat16)
        dhidden_part = lax.psum_scatter(
            jnp.einsum(
                "rlf,df->rld", dexpanded, expand_local, preferred_element_type=jnp.float32
            ).astype(jnp.bfloat16),
            "mp",
            scatter_dimension=0,
            tiled=True,
        ).astype(jnp.float32)
        dhidden = dsummed + dhidden_part
        dmixed = norm_backward(dhidden, gains[0], normed_one, scale_one)
        dmixed_low = dmixed.astype(jnp.bfloat16)
        full_dmixed = lax.all_gather(dmixed_low, "mp", axis=0, tiled=True)
        dcontext = jnp.einsum(
            "rld,ed->rle", full_dmixed, output_local, preferred_element_type=jnp.float32
        ).astype(jnp.bfloat16)
        dprojected = attend_back(projected, allowed, log_total, dcontext, head_count)
        dinput_part = lax.psum_scatter(
            jnp.einsum(
                "rlje,jde->rld", dprojected, triple_local, preferred_element_type=jnp.float32
            ).astype(jnp.bfloat16),
            "mp",
            scatter_dimension=0,
            tiled=True,
        ).astype(jnp.float32)
        input_grads.append(dmixed + dinput_part)
        triple_grad = triple_grad + jnp.einsum(
            "rld,rlje->jde", full_inputs, dprojected, preferred_element_type=jnp.float32
        )
        bias_grad = bias_grad + jnp.sum(dprojected, axis=(0, 1), dtype=jnp.float32)
        output_grad = output_grad + jnp.einsum(
            "rle,rld->ed", context, full_dmixed, preferred_element_type=jnp.float32
        )
        expand_grad = expand_grad + jnp.einsum(
            "rld,rlf->df", full_hidden, dexpanded, preferred_element_type=jnp.float32
        )
        expand_shift_grad = expand_shift_grad + jnp.sum(dexpanded, axis=(0, 1), dtype=jnp.float32)
        shrink_grad = shrink_grad + jnp.einsum(
            "rlf,rld->fd", active, full_dsummed, preferred_element_type=jnp.float32
        )
        vector_grad = vector_grad + jnp.stack(
            [
                jnp.sum(dhidden * normed_one, axis=(0, 1)),
                jnp.sum(dhidden, axis=(0, 1)),
                jnp.sum(dmixed, axis=(0, 1)),
                jnp.sum(own_back * normed_two, axis=(0, 1)),
                jnp.sum(own_back, axis=(0, 1)),
                jnp.sum(dsummed, axis=(0, 1)),
            ]
        )
    query_value_grad = jnp.stack([bias_grad[0], bias_grad[2]]).reshape(2, head_count, HEAD)
    expand_bias_grad = expand_shift_grad.reshape(-1, HEAD)
    gradients = (
        triple_grad,
        query_value_grad,
        output_grad,
        expand_grad,
        expand_bias_grad,
        shrink_grad,
    )
    gradients = (
        lax.psum_scatter(gradients[0], "dp", scatter_dimension=1, tiled=True),
        lax.psum_scatter(gradients[1], "dp", scatter_dimension=2, tiled=True),
        lax.psum_scatter(gradients[2], "dp", scatter_dimension=1, tiled=True),
        lax.psum_scatter(gradients[3], "dp", scatter_dimension=0, tiled=True),
        lax.psum_scatter(gradients[4], "dp", scatter_dimension=1, tiled=True),
        lax.psum_scatter(gradients[5], "dp", scatter_dimension=1, tiled=True),
    )
    vector_reduced = lax.psum_scatter(vector_grad, ("dp", "mp"), scatter_dimension=1, tiled=True)
    triple_out = adam_update(triple_master, triple_first, triple_second, gradients[0], D ** (-0.5))
    query_value_out = adam_update(
        query_value_master, query_value_first, query_value_second, gradients[1], 0.5
    )
    output_out = adam_update(
        output_master, output_first, output_second, gradients[2], (D // 16) ** (-0.5)
    )
    expand_out = adam_update(expand_master, expand_first, expand_second, gradients[3], D ** (-0.5))
    expand_bias_out = adam_update(
        expand_bias_master, expand_bias_first, expand_bias_second, gradients[4], 0.5
    )
    shrink_out = adam_update(shrink_master, shrink_first, shrink_second, gradients[5], FF ** (-0.5))
    vector_out = adam_update(vector_master, vector_first, vector_second, vector_reduced, 0.3)
    block_output = jnp.concatenate(outputs, axis=0)
    input_grad = jnp.concatenate(input_grads, axis=0)
    return (
        (block_output, input_grad)
        + triple_out
        + query_value_out
        + output_out
        + expand_out
        + expand_bias_out
        + shrink_out
        + vector_out
    )


def solution(mesh):
    placed = (
        P(("dp", "mp"), None, None),
        P(("dp", "mp"), None, None),
        P("dp", None),
        P(None, None, "mp"),
        P(None, "mp", None),
        P("mp", None),
        P(None, "mp"),
        P("mp", None),
        P("mp", None),
        P(),
        P(None, "dp", "mp"),
        P(None, "dp", "mp"),
        P(None, "dp", "mp"),
        P(None, "mp", "dp"),
        P(None, "mp", "dp"),
        P(None, "mp", "dp"),
        P("mp", "dp"),
        P("mp", "dp"),
        P("mp", "dp"),
        P("dp", "mp"),
        P("dp", "mp"),
        P("dp", "mp"),
        P("mp", "dp"),
        P("mp", "dp"),
        P("mp", "dp"),
        P("mp", "dp"),
        P("mp", "dp"),
        P("mp", "dp"),
        P(None, ("dp", "mp")),
        P(None, ("dp", "mp")),
        P(None, ("dp", "mp")),
    )
    return jax.shard_map(
        per_device,
        mesh=mesh,
        in_specs=placed,
        out_specs=(
            P(("dp", "mp"), None, None),
            P(("dp", "mp"), None, None),
            P(None, "dp", "mp"),
            P(None, "dp", "mp"),
            P(None, "dp", "mp"),
            P(None, "dp", "mp"),
            P(None, "mp", "dp"),
            P(None, "mp", "dp"),
            P(None, "mp", "dp"),
            P(None, "mp", "dp"),
            P("mp", "dp"),
            P("mp", "dp"),
            P("mp", "dp"),
            P("mp", "dp"),
            P("dp", "mp"),
            P("dp", "mp"),
            P("dp", "mp"),
            P("dp", "mp"),
            P("mp", "dp"),
            P("mp", "dp"),
            P("mp", "dp"),
            P("mp", "dp"),
            P("mp", "dp"),
            P("mp", "dp"),
            P("mp", "dp"),
            P("mp", "dp"),
            P(None, ("dp", "mp")),
            P(None, ("dp", "mp")),
            P(None, ("dp", "mp")),
            P(None, ("dp", "mp")),
        ),
        check_vma=False,
    )
```

profile of v0, /device:TPU:0, one launch (start us, length us, event | category | flops | bytes accessed | tf_op | source)
XLA Modules:
  0.0 1532.0 jit_solution(792180418235632875)
XLA Ops:
  12.9 40.4 %all-gather.17.cloned.1.call-done = bf16[4,288,768]{2,1,0:T(8,128)(2,1)} async-done(((bf16[1,288,768]{2,1,0:T(8,128)(2,1)}), bf16[4,288,768]{2,1,0:T(8,128)(2,1)}) %all-gather.17.cloned.1.call-update) | async-done | bytes 1769488 | tf_op jit(solution)/shard_map/all_gather | solution.py:165
  64.1 30.5 %all-gather.21.cloned.1.call-done = bf16[4,288,768]{2,1,0:T(8,128)(2,1)} async-done(((bf16[1,288,768]{2,1,0:T(8,128)(2,1)}), bf16[4,288,768]{2,1,0:T(8,128)(2,1)}) %all-gather.21.cloned.1.call-update) | async-done | bytes 1769488 | tf_op jit(solution)/shard_map/all_gather | solution.py:165
  105.7 29.8 %all-gather.29.cloned.1.call-done = bf16[4,288,768]{2,1,0:T(8,128)(2,1)} async-done(((bf16[1,288,768]{2,1,0:T(8,128)(2,1)}), bf16[4,288,768]{2,1,0:T(8,128)(2,1)}) %all-gather.29.cloned.1.call-update) | async-done | bytes 1769488 | tf_op jit(solution)/shard_map/all_gather | solution.py:165
  146.7 28.8 %reduce-scatter.28.cloned.1.call-done = bf16[1,288,768]{2,1,0:T(8,128)(2,1)} async-done(((bf16[4,288,768]{2,1,0:T(8,128)(2,1)}), bf16[1,288,768]{2,1,0:T(8,128)(2,1)}) %reduce-scatter.28.cloned.1.call-update) | async-done | bytes 442384 | tf_op jit(solution)/shard_map/reduce_scatter | solution.py:173
  177.3 38.5 %reduce-scatter.32.cloned.1.call-done = bf16[1,288,768]{2,1,0:T(8,128)(2,1)} async-done(((bf16[4,288,768]{2,1,0:T(8,128)(2,1)}), bf16[1,288,768]{2,1,0:T(8,128)(2,1)}) %reduce-scatter.32.cloned.1.call-update) | async-done | bytes 442384 | tf_op jit(solution)/shard_map/reduce_scatter | solution.py:173
  215.9 39.7 %reduce-scatter.40.cloned.1.call-done = bf16[1,288,768]{2,1,0:T(8,128)(2,1)} async-done(((bf16[4,288,768]{2,1,0:T(8,128)(2,1)}), bf16[1,288,768]{2,1,0:T(8,128)(2,1)}) %reduce-scatter.40.cloned.1.call-update) | async-done | bytes 442384 | tf_op jit(solution)/shard_map/reduce_scatter | solution.py:173
  263.9 37.4 %all-gather.23.cloned.1.call-done = bf16[4,288,768]{2,1,0:T(8,128)(2,1)} async-done(((bf16[1,288,768]{2,1,0:T(8,128)(2,1)}), bf16[4,288,768]{2,1,0:T(8,128)(2,1)}) %all-gather.23.cloned.1.call-update) | async-done | bytes 1769488 | tf_op jit(solution)/shard_map/all_gather | solution.py:184
  301.3 4.8 fusion.118
  306.1 36.6 %all-gather.19.cloned.1.call-done = bf16[4,288,768]{2,1,0:T(8,128)(2,1)} async-done(((bf16[1,288,768]{2,1,0:T(8,128)(2,1)}), bf16[4,288,768]{2,1,0:T(8,128)(2,1)}) %all-gather.19.cloned.1.call-update) | async-done | bytes 1769488 | tf_op jit(solution)/shard_map/all_gather | solution.py:184
  342.7 6.5 multiply_convert_fusion.7
  353.3 4.6 convolution_convert_fusion.10
  359.6 31.1 %reduce-scatter.30.cloned.1.call-done = bf16[1,288,768]{2,1,0:T(8,128)(2,1)} async-done(((bf16[4,288,768]{2,1,0:T(8,128)(2,1)}), bf16[1,288,768]{2,1,0:T(8,128)(2,1)}) %reduce-scatter.30.cloned.1.call-update) | async-done | bytes 442384 | tf_op jit(solution)/shard_map/reduce_scatter | solution.py:190
  390.7 39.7 %reduce-scatter.34.cloned.1.call-done = bf16[1,288,768]{2,1,0:T(8,128)(2,1)} async-done(((bf16[4,288,768]{2,1,0:T(8,128)(2,1)}), bf16[1,288,768]{2,1,0:T(8,128)(2,1)}) %reduce-scatter.34.cloned.1.call-update) | async-done | bytes 442384 | tf_op jit(solution)/shard_map/reduce_scatter | solution.py:190
  430.4 4.3 fusion.205
  434.8 39.5 %all-gather.31.cloned.1.call-done = bf16[4,288,768]{2,1,0:T(8,128)(2,1)} async-done(((bf16[1,288,768]{2,1,0:T(8,128)(2,1)}), bf16[4,288,768]{2,1,0:T(8,128)(2,1)}) %all-gather.31.cloned.1.call-update) | async-done | bytes 1769488 | tf_op jit(solution)/shard_map/all_gather | solution.py:184
  474.3 5.2 multiply_convert_fusion.4
  489.9 31.0 %reduce-scatter.42.cloned.1.call-done = bf16[1,288,768]{2,1,0:T(8,128)(2,1)} async-done(((bf16[4,288,768]{2,1,0:T(8,128)(2,1)}), bf16[1,288,768]{2,1,0:T(8,128)(2,1)}) %reduce-scatter.42.cloned.1.call-update) | async-done | bytes 442384 | tf_op jit(solution)/shard_map/reduce_scatter | solution.py:190
  523.0 4.4 fusion.137
  532.3 29.7 %all-gather.25.cloned.1.call-done = bf16[4,288,768]{2,1,0:T(8,128)(2,1)} async-done(((bf16[1,288,768]{2,1,0:T(8,128)(2,1)}), bf16[4,288,768]{2,1,0:T(8,128)(2,1)}) %all-gather.25.cloned.1.call-update) | async-done | bytes 1769488 | tf_op jit(solution)/shard_map/all_gather | solution.py:165
  573.0 29.6 %all-gather.37.cloned.1.call-done = bf16[4,288,768]{2,1,0:T(8,128)(2,1)} async-done(((bf16[1,288,768]{2,1,0:T(8,128)(2,1)}), bf16[4,288,768]{2,1,0:T(8,128)(2,1)}) %all-gather.37.cloned.1.call-update) | async-done | bytes 1769488 | tf_op jit(solution)/shard_map/all_gather | solution.py:203
  602.6 5.9 convert_reduce_fusion.2
  612.6 30.6 %all-gather.45.cloned.1.call-done = bf16[4,288,768]{2,1,0:T(8,128)(2,1)} async-done(((bf16[1,288,768]{2,1,0:T(8,128)(2,1)}), bf16[4,288,768]{2,1,0:T(8,128)(2,1)}) %all-gather.45.cloned.1.call-update) | async-done | bytes 1769488 | tf_op jit(solution)/shard_map/all_gather | solution.py:203
  643.3 5.9 convert_reduce_fusion
  653.3 29.4 %reduce-scatter.36.cloned.1.call-done = bf16[1,288,768]{2,1,0:T(8,128)(2,1)} async-done(((bf16[4,288,768]{2,1,0:T(8,128)(2,1)}), bf16[1,288,768]{2,1,0:T(8,128)(2,1)}) %reduce-scatter.36.cloned.1.call-update) | async-done | bytes 442384 | tf_op jit(solution)/shard_map/reduce_scatter | solution.py:173
  682.7 39.8 %reduce-scatter.48.cloned.1.call-done = bf16[1,288,768]{2,1,0:T(8,128)(2,1)} async-done(((bf16[4,288,768]{2,1,0:T(8,128)(2,1)}), bf16[1,288,768]{2,1,0:T(8,128)(2,1)}) %reduce-scatter.48.cloned.1.call-update) | async-done | bytes 442384 | tf_op jit(solution)/shard_map/reduce_scatter | solution.py:208
  722.6 40.3 %reduce-scatter.56.cloned.1.call-done = bf16[1,288,768]{2,1,0:T(8,128)(2,1)} async-done(((bf16[4,288,768]{2,1,0:T(8,128)(2,1)}), bf16[1,288,768]{2,1,0:T(8,128)(2,1)}) %reduce-scatter.56.cloned.1.call-update) | async-done | bytes 442384 | tf_op jit(solution)/shard_map/reduce_scatter | solution.py:208
  762.8 4.0 multiply_reduce_fusion.4
  769.1 39.5 %all-gather.27.cloned.1.call-done = bf16[4,288,768]{2,1,0:T(8,128)(2,1)} async-done(((bf16[1,288,768]{2,1,0:T(8,128)(2,1)}), bf16[4,288,768]{2,1,0:T(8,128)(2,1)}) %all-gather.27.cloned.1.call-update) | async-done | bytes 1769488 | tf_op jit(solution)/shard_map/all_gather | solution.py:184
  808.6 5.2 multiply_convert_fusion.5
  818.9 36.2 %reduce-scatter.38.cloned.1.call-done = bf16[1,288,768]{2,1,0:T(8,128)(2,1)} async-done(((bf16[4,288,768]{2,1,0:T(8,128)(2,1)}), bf16[1,288,768]{2,1,0:T(8,128)(2,1)}) %reduce-scatter.38.cloned.1.call-update) | async-done | bytes 442384 | tf_op jit(solution)/shard_map/reduce_scatter | solution.py:190
  860.2 36.0 %all-gather.33.cloned.1.call-done = bf16[4,288,768]{2,1,0:T(8,128)(2,1)} async-done(((bf16[1,288,768]{2,1,0:T(8,128)(2,1)}), bf16[4,288,768]{2,1,0:T(8,128)(2,1)}) %all-gather.33.cloned.1.call-update) | async-done | bytes 1769488 | tf_op jit(solution)/shard_map/all_gather | solution.py:203
  896.2 5.9 convert_reduce_fusion.3
  906.3 30.7 %all-gather.41.cloned.1.call-done = bf16[4,288,768]{2,1,0:T(8,128)(2,1)} async-done(((bf16[1,288,768]{2,1,0:T(8,128)(2,1)}), bf16[4,288,768]{2,1,0:T(8,128)(2,1)}) %all-gather.41.cloned.1.call-update) | async-done | bytes 1769488 | tf_op jit(solution)/shard_map/all_gather | solution.py:203
  937.0 5.9 convert_reduce_fusion.1
  947.6 29.0 %reduce-scatter.44.cloned.1.call-done = bf16[1,288,768]{2,1,0:T(8,128)(2,1)} async-done(((bf16[4,288,768]{2,1,0:T(8,128)(2,1)}), bf16[1,288,768]{2,1,0:T(8,128)(2,1)}) %reduce-scatter.44.cloned.1.call-update) | async-done | bytes 442384 | tf_op jit(solution)/shard_map/reduce_scatter | solution.py:208
  976.6 40.4 %reduce-scatter.52.cloned.1.call-done = bf16[1,288,768]{2,1,0:T(8,128)(2,1)} async-done(((bf16[4,288,768]{2,1,0:T(8,128)(2,1)}), bf16[1,288,768]{2,1,0:T(8,128)(2,1)}) %reduce-scatter.52.cloned.1.call-update) | async-done | bytes 442384 | tf_op jit(solution)/shard_map/reduce_scatter | solution.py:208
  1017.1 3.7 multiply_reduce_fusion.5
  1027.5 3.9 fusion.182
  1034.1 3.9 fusion.216
  1046.5 3.9 fusion.218
  1058.2 6.4 all-gather.39.cloned.1.call-done
  1066.9 4.5 fusion.78
  1071.5 4.2 multiply_reduce_fusion.2
  1080.2 25.1 %all-gather.43.cloned.1.call-done = bf16[4,288,768]{2,1,0:T(8,128)(2,1)} async-done(((bf16[1,288,768]{2,1,0:T(8,128)(2,1)}), bf16[4,288,768]{2,1,0:T(8,128)(2,1)}) %all-gather.43.cloned.1.call-update) | async-done | bytes 1769488 | tf_op jit(solution)/shard_map/all_gather | solution.py:219
  1107.6 4.5 fusion.81
  1112.1 4.2 multiply_reduce_fusion.1
  1120.8 25.1 %all-gather.35.cloned.1.call-done = bf16[4,288,768]{2,1,0:T(8,128)(2,1)} async-done(((bf16[1,288,768]{2,1,0:T(8,128)(2,1)}), bf16[4,288,768]{2,1,0:T(8,128)(2,1)}) %all-gather.35.cloned.1.call-update) | async-done | bytes 1769488 | tf_op jit(solution)/shard_map/all_gather | solution.py:219
  1148.2 4.4 fusion.75
  1152.6 34.1 %all-gather.47.cloned.1.call-done = bf16[4,288,768]{2,1,0:T(8,128)(2,1)} async-done(((bf16[1,288,768]{2,1,0:T(8,128)(2,1)}), bf16[4,288,768]{2,1,0:T(8,128)(2,1)}) %all-gather.47.cloned.1.call-update) | async-done | bytes 1769488 | tf_op jit(solution)/shard_map/all_gather | solution.py:219
  1189.0 4.7 fusion.84
  1220.2 4.1 multiply_reduce_fusion
  1233.2 4.1 multiply_reduce_fusion.3
  1257.2 4.2 copy.360
  1261.4 4.7 reshape.604
  1266.2 4.6 bitcast_convert_fusion.2
  1270.9 4.4 bitcast_convert_fusion.1
  1275.7 4.4 bitcast_convert_fusion
  1290.6 39.5 %all-reduce.2 = f32[6,768]{1,0:T(8,128)S(1)} all-reduce(f32[6,768]{1,0:T(8,128)S(1)} %add_add_fusion.8), channel_id=24, replica_groups=mesh['dp'=8,'mp'=4] {'dp','mp'}, use_global_device_ids=true, to_apply=%region_98.99.clone | all-reduce | flops 4608 | bytes 36864
  1330.8 4.5 bitcast_convert_fusion.3
  1344.8 23.4 %all-reduce.3 = (f32[2,3,64]{2,1,0:T(4,128)S(1)}, f32[12,64]{1,0:T(8,128)S(1)}) all-reduce(f32[2,3,64]{2,1,0:T(4,128)S(1)} %reshape.574, f32[12,64]{1,0:T(8,128)S(1)} %add.676), channel_id=19, replica_groups=mesh['dp'=8,'mp'=4] {'dp'}, use_global_device_ids=true, to_apply=%region_65.66.clone | all-reduce | flops 1152 | bytes 9216
  1381.6 18.7 %reduce-scatter.50.cloned.1.call-done = bf16[1,288,768]{2,1,0:T(8,128)(2,1)} async-done(((bf16[4,288,768]{2,1,0:T(8,128)(2,1)}), bf16[1,288,768]{2,1,0:T(8,128)(2,1)}) %reduce-scatter.50.cloned.1.call-update) | async-done | bytes 442384 | tf_op jit(solution)/shard_map/reduce_scatter | solution.py:224
  1402.3 37.8 %reduce-scatter.54.cloned.1.call-done = bf16[1,288,768]{2,1,0:T(8,128)(2,1)} async-done(((bf16[4,288,768]{2,1,0:T(8,128)(2,1)}), bf16[1,288,768]{2,1,0:T(8,128)(2,1)}) %reduce-scatter.54.cloned.1.call-update) | async-done | bytes 442384 | tf_op jit(solution)/shard_map/reduce_scatter | solution.py:224
  1442.2 38.5 %reduce-scatter.58.cloned.1.call-done = bf16[1,288,768]{2,1,0:T(8,128)(2,1)} async-done(((bf16[4,288,768]{2,1,0:T(8,128)(2,1)}), bf16[1,288,768]{2,1,0:T(8,128)(2,1)}) %reduce-scatter.58.cloned.1.call-update) | async-done | bytes 442384 | tf_op jit(solution)/shard_map/reduce_scatter | solution.py:224
  1482.7 37.7 %reduce-scatter.46.cloned.1.call-done = bf16[1,288,768]{2,1,0:T(8,128)(2,1)} async-done(((bf16[4,288,768]{2,1,0:T(8,128)(2,1)}), bf16[1,288,768]{2,1,0:T(8,128)(2,1)}) %reduce-scatter.46.cloned.1.call-update) | async-done | bytes 442384 | tf_op jit(solution)/shard_map/reduce_scatter | solution.py:224
  (674 shorter events, 253.8 us)
Async XLA Ops:
  7.2 294.1 %copy-start = (bf16[768,768]{1,0:T(8,128)(2,1)S(1)}, bf16[768,768]{1,0:T(8,128)(2,1)}, u32[]{:S(2)}) copy-start(bf16[768,768]{1,0:T(8,128)(2,1)} %param.37) | copy-start | bytes 3538948
  7.2 46.0 %all-gather.17.cloned.1.call-start = ((), (), s32[]{:S(2)}) async-start(), calls=%async_computation.20 | async-start | bytes 2211840 | tf_op jit(solution)/shard_map/all_gather | solution.py:165
  10.0 43.2 %copy-start.169 = (bf16[3,768,192]{1,2,0:T(8,128)(2,1)S(1)}, bf16[3,768,192]{1,2,0:T(8,128)(2,1)}, u32[]{:S(2)}) copy-start(bf16[3,768,192]{1,2,0:T(8,128)(2,1)} %param.34) | copy-start | bytes 2654212
  10.1 84.6 %all-gather.21.cloned.1.call-start = ((), (), s32[]{:S(2)}) async-start(), calls=%async_computation.24 | async-start | bytes 2211840 | tf_op jit(solution)/shard_map/all_gather | solution.py:165
  10.8 124.6 %all-gather.29.cloned.1.call-start = ((), (), s32[]{:S(2)}) async-start(), calls=%async_computation.32 | async-start | bytes 2211840 | tf_op jit(solution)/shard_map/all_gather | solution.py:165
  11.5 163.9 %reduce-scatter.28.cloned.1.call-start = ((), (), s32[]{:S(2)}) async-start(), calls=%async_computation.21 | async-start | bytes 2211840 | tf_op jit(solution)/shard_map/reduce_scatter | solution.py:173
  12.6 122.9 %copy-start.150 = (f32[3,192]{1,0:T(4,128)}, f32[3,192]{1,0:T(4,128)S(1)}, u32[]{:S(2)}) copy-start(f32[3,192]{1,0:T(4,128)S(1)} %pad_maximum_fusion.6) | copy-start | bytes 6916
  63.8 152.1 %reduce-scatter.32.cloned.1.call-start = ((), (), s32[]{:S(2)}) async-start(), calls=%async_computation.25 | async-start | bytes 2211840 | tf_op jit(solution)/shard_map/reduce_scatter | solution.py:173
  105.1 150.5 %reduce-scatter.40.cloned.1.call-start = ((), (), s32[]{:S(2)}) async-start(), calls=%async_computation.33 | async-start | bytes 2211840 | tf_op jit(solution)/shard_map/reduce_scatter | solution.py:173
  144.0 31.4 %copy-start.2 = (bf16[4,288,768]{2,1,0:T(8,128)(2,1)S(1)}, bf16[4,288,768]{2,1,0:T(8,128)(2,1)}, u32[]{:S(2)}) copy-start(bf16[4,288,768]{2,1,0:T(8,128)(2,1)} %param.31) | copy-start | bytes 5308420
  146.0 155.3 %all-gather.23.cloned.1.call-start = ((), (), s32[]{:S(2)}) async-start(), calls=%async_computation.26 | async-start | bytes 2211840 | tf_op jit(solution)/shard_map/all_gather | solution.py:184
  261.7 81.0 %all-gather.19.cloned.1.call-start = ((), (), s32[]{:S(2)}) async-start(), calls=%async_computation.22 | async-start | bytes 2211840 | tf_op jit(solution)/shard_map/all_gather | solution.py:184
  262.5 128.2 %reduce-scatter.30.cloned.1.call-start = ((), (), s32[]{:S(2)}) async-start(), calls=%async_computation.23 | async-start | bytes 2211840 | tf_op jit(solution)/shard_map/reduce_scatter | solution.py:190
  353.3 77.1 %reduce-scatter.34.cloned.1.call-start = ((), (), s32[]{:S(2)}) async-start(), calls=%async_computation.27 | async-start | bytes 2211840 | tf_op jit(solution)/shard_map/reduce_scatter | solution.py:190
  357.9 116.4 %all-gather.31.cloned.1.call-start = ((), (), s32[]{:S(2)}) async-start(), calls=%async_computation.34 | async-start | bytes 2211840 | tf_op jit(solution)/shard_map/all_gather | solution.py:184
  434.7 86.2 %reduce-scatter.42.cloned.1.call-start = ((), (), s32[]{:S(2)}) async-start(), calls=%async_computation.35 | async-start | bytes 2211840 | tf_op jit(solution)/shard_map/reduce_scatter | solution.py:190
  483.5 78.4 %all-gather.25.cloned.1.call-start = ((), (), s32[]{:S(2)}) async-start(), calls=%async_computation.28 | async-start | bytes 2211840 | tf_op jit(solution)/shard_map/all_gather | solution.py:165
  484.3 118.3 %all-gather.37.cloned.1.call-start = ((), (), s32[]{:S(2)}) async-start(), calls=%async_computation.40 | async-start | bytes 2211840 | tf_op jit(solution)/shard_map/all_gather | solution.py:203
  529.8 113.4 %all-gather.45.cloned.1.call-start = ((), (), s32[]{:S(2)}) async-start(), calls=%async_computation.48 | async-start | bytes 2211840 | tf_op jit(solution)/shard_map/all_gather | solution.py:203
  530.4 152.3 %reduce-scatter.36.cloned.1.call-start = ((), (), s32[]{:S(2)}) async-start(), calls=%async_computation.29 | async-start | bytes 2211840 | tf_op jit(solution)/shard_map/reduce_scatter | solution.py:173
  572.8 149.7 %reduce-scatter.48.cloned.1.call-start = ((), (), s32[]{:S(2)}) async-start(), calls=%async_computation.41 | async-start | bytes 2211840 | tf_op jit(solution)/shard_map/reduce_scatter | solution.py:208
  612.6 150.2 %reduce-scatter.56.cloned.1.call-start = ((), (), s32[]{:S(2)}) async-start(), calls=%async_computation.49 | async-start | bytes 2211840 | tf_op jit(solution)/shard_map/reduce_scatter | solution.py:208
  653.3 155.3 %all-gather.27.cloned.1.call-start = ((), (), s32[]{:S(2)}) async-start(), calls=%async_computation.30 | async-start | bytes 2211840 | tf_op jit(solution)/shard_map/all_gather | solution.py:184
  769.0 86.1 %reduce-scatter.38.cloned.1.call-start = ((), (), s32[]{:S(2)}) async-start(), calls=%async_computation.31 | async-start | bytes 2211840 | tf_op jit(solution)/shard_map/reduce_scatter | solution.py:190
  817.7 78.4 %all-gather.33.cloned.1.call-start = ((), (), s32[]{:S(2)}) async-start(), calls=%async_computation.36 | async-start | bytes 2211840 | tf_op jit(solution)/shard_map/all_gather | solution.py:203
  818.4 118.5 %all-gather.41.cloned.1.call-start = ((), (), s32[]{:S(2)}) async-start(), calls=%async_computation.44 | async-start | bytes 2211840 | tf_op jit(solution)/shard_map/all_gather | solution.py:203
  860.1 116.5 %reduce-scatter.44.cloned.1.call-start = ((), (), s32[]{:S(2)}) async-start(), calls=%async_computation.37 | async-start | bytes 2211840 | tf_op jit(solution)/shard_map/reduce_scatter | solution.py:208
  906.2 30.8 %copy-start.149 = (f32[768]{0:T(1024)S(1)}, f32[768]{0:T(1024)}, u32[]{:S(2)}) copy-start(f32[768]{0:T(1024)} %reshape.575) | copy-start | bytes 9220
  906.2 110.7 %reduce-scatter.52.cloned.1.call-start = ((), (), s32[]{:S(2)}) async-start(), calls=%async_computation.45 | async-start | bytes 2211840 | tf_op jit(solution)/shard_map/reduce_scatter | solution.py:208
  946.9 70.1 %copy-start.15 = (bf16[1,288,768]{2,1,0:T(8,128)(2,1)S(1)}, bf16[1,288,768]{2,1,0:T(8,128)(2,1)}, u32[]{:S(2)}) copy-start(bf16[1,288,768]{2,1,0:T(8,128)(2,1)} %reduce-scatter.36.cloned.1.call-done) | copy-start | bytes 1327108
  946.9 70.1 %copy-start.91 = (f32[288]{0:T(512)S(1)}, f32[288]{0:T(512)}, u32[]{:S(2)}) copy-start(f32[288]{0:T(512)} %copy-done.90) | copy-start | bytes 3460
  946.9 70.1 %copy-start.93 = (f32[288]{0:T(512)S(1)}, f32[288]{0:T(512)}, u32[]{:S(2)}) copy-start(f32[288]{0:T(512)} %broadcast_multiply_fusion.30) | copy-start | bytes 3460
  946.9 70.1 %copy-start.98 = (f32[288]{0:T(512)S(1)}, f32[288]{0:T(512)}, u32[]{:S(2)}) copy-start(f32[288]{0:T(512)} %copy-done.97) | copy-start | bytes 3460
  946.9 70.1 %copy-start.100 = (f32[288]{0:T(512)S(1)}, f32[288]{0:T(512)}, u32[]{:S(2)}) copy-start(f32[288]{0:T(512)} %copy-done.99) | copy-start | bytes 3460
  947.0 117.7 %all-gather.39.cloned.1.call-start = ((), (), s32[]{:S(2)}) async-start(), calls=%async_computation.42 | async-start | bytes 2211840 | tf_op jit(solution)/shard_map/all_gather | solution.py:219
  1025.1 80.2 %all-gather.43.cloned.1.call-start = ((), (), s32[]{:S(2)}) async-start(), calls=%async_computation.46 | async-start | bytes 2211840 | tf_op jit(solution)/shard_map/all_gather | solution.py:219
  1027.1 118.8 %all-gather.35.cloned.1.call-start = ((), (), s32[]{:S(2)}) async-start(), calls=%async_computation.38 | async-start | bytes 2211840 | tf_op jit(solution)/shard_map/all_gather | solution.py:219
  1033.2 153.6 %all-gather.47.cloned.1.call-start = ((), (), s32[]{:S(2)}) async-start(), calls=%async_computation.50 | async-start | bytes 2211840 | tf_op jit(solution)/shard_map/all_gather | solution.py:219
  1034.1 301.2 %reduce-scatter.60.cloned.1.call-start = ((), (), s32[]{:S(2)}) async-start(), calls=%async_computation.52 | async-start | bytes 2654208 | tf_op jit(solution)/shard_map/reduce_scatter | solution.py:271
  1045.6 292.9 %reduce-scatter.62.cloned.1.call-start = ((), (), s32[]{:S(2)}) async-start(), calls=%async_computation.53 | async-start | bytes 2654208 | tf_op jit(solution)/shard_map/reduce_scatter | solution.py:273
  1057.8 313.6 %reduce-scatter.66.cloned.1.call-start = ((), (), s32[]{:S(2)}) async-start(), calls=%async_computation.55 | async-start | bytes 884736
  1246.6 126.6 %reduce-scatter.64.cloned.1.call-start = ((), (), s32[]{:S(2)}) async-start(), calls=%async_computation.54 | async-start | bytes 2211840
  1266.2 134.2 %reduce-scatter.50.cloned.1.call-start = ((), (), s32[]{:S(2)}) async-start(), calls=%async_computation.43 | async-start | bytes 2211840 | tf_op jit(solution)/shard_map/reduce_scatter | solution.py:224
  1270.9 169.3 %reduce-scatter.54.cloned.1.call-start = ((), (), s32[]{:S(2)}) async-start(), calls=%async_computation.47 | async-start | bytes 2211840 | tf_op jit(solution)/shard_map/reduce_scatter | solution.py:224
  1275.4 205.3 %reduce-scatter.58.cloned.1.call-start = ((), (), s32[]{:S(2)}) async-start(), calls=%async_computation.51 | async-start | bytes 2211840 | tf_op jit(solution)/shard_map/reduce_scatter | solution.py:224
  1280.3 240.1 %reduce-scatter.46.cloned.1.call-start = ((), (), s32[]{:S(2)}) async-start(), calls=%async_computation.39 | async-start | bytes 2211840 | tf_op jit(solution)/shard_map/reduce_scatter | solution.py:224
  1287.3 42.7 %copy-start.139 = (f32[6,24]{1,0:T(8,128)S(1)}, f32[6,24]{1,0:T(8,128)}, u32[]{:S(2)}) copy-start(f32[6,24]{1,0:T(8,128)} %param.59) | copy-start | bytes 1732
  1287.3 42.7 %copy-start.140 = (f32[6,24]{1,0:T(8,128)S(1)}, f32[6,24]{1,0:T(8,128)}, u32[]{:S(2)}) copy-start(f32[6,24]{1,0:T(8,128)} %param.60) | copy-start | bytes 1732
  1287.3 42.7 %copy-start.141 = (f32[6,24]{1,0:T(8,128)S(1)}, f32[6,24]{1,0:T(8,128)}, u32[]{:S(2)}) copy-start(f32[6,24]{1,0:T(8,128)} %param.61) | copy-start | bytes 1732
  1343.5 24.8 %copy-start.151 = (f32[2,3,8]{2,0,1:T(2,128)S(1)}, f32[2,3,8]{2,0,1:T(2,128)}, u32[]{:S(2)}) copy-start(f32[2,3,8]{2,0,1:T(2,128)} %param.45) | copy-start | bytes 580
  1343.5 24.8 %copy-start.152 = (f32[2,3,8]{2,0,1:T(2,128)S(1)}, f32[2,3,8]{2,0,1:T(2,128)}, u32[]{:S(2)}) copy-start(f32[2,3,8]{2,0,1:T(2,128)} %param.44) | copy-start | bytes 580
  1343.5 24.8 %copy-start.153 = (f32[2,3,8]{2,0,1:T(2,128)S(1)}, f32[2,3,8]{2,0,1:T(2,128)}, u32[]{:S(2)}) copy-start(f32[2,3,8]{2,0,1:T(2,128)} %param.46) | copy-start | bytes 580
  1343.5 27.2 %copy-start.142 = (f32[12,8]{0,1:T(8,128)S(1)}, f32[12,8]{0,1:T(8,128)}, u32[]{:S(2)}) copy-start(f32[12,8]{0,1:T(8,128)} %param.53) | copy-start | bytes 1156
  1343.5 27.2 %copy-start.143 = (f32[12,8]{0,1:T(8,128)S(1)}, f32[12,8]{0,1:T(8,128)}, u32[]{:S(2)}) copy-start(f32[12,8]{0,1:T(8,128)} %param.54) | copy-start | bytes 1156
  1343.5 27.2 %copy-start.144 = (f32[12,8]{0,1:T(8,128)S(1)}, f32[12,8]{0,1:T(8,128)}, u32[]{:S(2)}) copy-start(f32[12,8]{0,1:T(8,128)} %param.55) | copy-start | bytes 1156
  1343.6 28.8 %copy-start.83 = (f32[192,96]{1,0:T(8,128)S(1)}, f32[192,96]{1,0:T(8,128)}, u32[]{:S(2)}) copy-start(f32[192,96]{1,0:T(8,128)} %param.47) | copy-start | bytes 221188
  1343.6 28.8 %copy-start.84 = (f32[192,96]{1,0:T(8,128)S(1)}, f32[192,96]{1,0:T(8,128)}, u32[]{:S(2)}) copy-start(f32[192,96]{1,0:T(8,128)} %param.48) | copy-start | bytes 221188
  1343.6 28.8 %copy-start.85 = (f32[192,96]{1,0:T(8,128)S(1)}, f32[192,96]{1,0:T(8,128)}, u32[]{:S(2)}) copy-start(f32[192,96]{1,0:T(8,128)} %param.49) | copy-start | bytes 221188
  1344.3 30.9 %copy-start.69 = (f32[3,96,192]{1,2,0:T(8,128)S(1)}, f32[3,96,192]{1,2,0:T(8,128)}, u32[]{:S(2)}) copy-start(f32[3,96,192]{1,2,0:T(8,128)} %copy.309) | copy-start | bytes 663556
  1344.3 30.9 %copy-start.70 = (f32[3,96,192]{1,2,0:T(8,128)S(1)}, f32[3,96,192]{1,2,0:T(8,128)}, u32[]{:S(2)}) copy-start(f32[3,96,192]{1,2,0:T(8,128)} %copy.310) | copy-start | bytes 663556
  1375.2 25.1 %copy-start.24 = (f32[1,288,768]{2,1,0:T(8,128)S(1)}, f32[1,288,768]{2,1,0:T(8,128)}, u32[]{:S(2)}) copy-start(f32[1,288,768]{2,1,0:T(8,128)} %copy-done.23) | copy-start | bytes 2654212
  1378.9 61.3 %copy-start.22 = (f32[1,288,768]{2,1,0:T(8,128)S(1)}, f32[1,288,768]{2,1,0:T(8,128)}, u32[]{:S(2)}) copy-start(f32[1,288,768]{2,1,0:T(8,128)} %get-tuple-element.265) | copy-start | bytes 2654212
  1402.3 118.1 %copy-start.26 = (f32[1,288,768]{2,1,0:T(8,128)S(1)}, f32[1,288,768]{2,1,0:T(8,128)}, u32[]{:S(2)}) copy-start(f32[1,288,768]{2,1,0:T(8,128)} %copy-done.25) | copy-start | bytes 2654212
  1482.7 38.9 %copy-start.32 = (f32[1,288,768]{2,1,0:T(8,128)S(1)}, f32[1,288,768]{2,1,0:T(8,128)}, u32[]{:S(2)}) copy-start(f32[1,288,768]{2,1,0:T(8,128)} %convert_add_fusion.2) | copy-start | bytes 2654212
  (162 other events, 502.7 us)
Sparse Core Ops, SparseCore 0:
  10.2 43.0 all-gather.16
  55.4 39.1 all-gather.20
  96.2 39.1 all-gather.28
  138.2 37.2 reduce-scatter.27
  178.3 37.4 reduce-scatter.31
  218.0 37.4 reduce-scatter.39
  261.8 39.4 all-gather.22
  303.5 39.1 all-gather.18
  353.4 37.2 reduce-scatter.29
  392.8 37.4 reduce-scatter.33
  434.8 39.4 all-gather.30
  483.7 37.2 reduce-scatter.41
  522.5 39.4 all-gather.24
  563.4 39.1 all-gather.36
  604.0 39.1 all-gather.44
  645.4 37.2 reduce-scatter.35
  685.0 37.4 reduce-scatter.47
  725.3 37.4 reduce-scatter.55
  769.1 39.4 all-gather.26
  817.8 37.2 reduce-scatter.37
  856.7 39.4 all-gather.32
  897.7 39.1 all-gather.40
  939.3 37.2 reduce-scatter.43
  979.4 37.4 reduce-scatter.51
  1025.2 39.4 all-gather.38
  1066.1 39.1 all-gather.42
  1106.7 39.1 all-gather.34
  1147.5 39.1 all-gather.46
  1190.1 41.3 reduce-scatter.59
  1235.1 42.4 reduce-scatter.61
  1280.7 35.0 reduce-scatter.65
  1319.3 40.3 reduce-scatter.63
  1361.9 38.3 reduce-scatter.49
  1402.7 37.4 reduce-scatter.53
  1443.2 37.4 reduce-scatter.57
  1482.9 37.4 reduce-scatter.45
where the time goes:
time: 1540 us; the launch traced here: 1530 us
  waiting for transfers between devices  1060 us (69%)
  matrix products  212 us (14%)
  other arithmetic  88 us (6%)
  local copies, waits for them, and re-layouts  85.2 us (6%)
  blocking collectives  62.8 us (4%)
  between operations  17.8 us (1%)
    all_gather x4, waiting for transfers between devices, per_device(): full_hidden = lax.all_gather(hidden_low, 'mp', axis=0, tiled=True)  153 us
    reduce_scatter x4, waiting for transfers between devices, per_device(): lax.psum_scatter(jnp.einsum('rlf,df->rld', dexpanded, expand_local, prefe...  149 us
    reduce_scatter x4, waiting for transfers between devices, per_device(): lax.psum_scatter(jnp.einsum('rlf,fd->rld', active, shrink_local, preferre...  138 us
    reduce_scatter x4, waiting for transfers between devices, per_device(): lax.psum_scatter(jnp.einsum('rle,ed->rld', context, output_local, preferr...  136 us
    reduce_scatter x4, waiting for transfers between devices, per_device(): lax.psum_scatter(jnp.einsum('rlje,jde->rld', dprojected, triple_local, pr...  133 us
    all_gather x4, waiting for transfers between devices, per_device(): full_inputs = lax.all_gather(own_inputs, 'mp', axis=0, tiled=True)  130 us
    all_gather x4, waiting for transfers between devices, per_device(): full_dsummed = lax.all_gather(dsummed_low, 'mp', axis=0, tiled=True)  127 us
    all_gather x4, waiting for transfers between devices, per_device(): full_dmixed = lax.all_gather(dmixed_low, 'mp', axis=0, tiled=True)  90.7 us
  transfers between devices with their start and end apart: 36, of which 32 were waited for; matrix products, arithmetic and copies ran while one was open for 19% of the time, Pallas kernels for 0%

commit v1 on v0

v1 whole, which is shorter than its diff:
```python
import jax
import jax.numpy as jnp
from jax import lax
from jax.sharding import PartitionSpec as P

D = 768
HEAD = 64
FF = 3072
STEP = 10


NORM_EPS = 1e-05
BETA_ONE = 0.5
BETA_TWO = 0.6
ADAM_EPS = 1e-08
WEIGHT_DECAY = 0.01
MASKED = -1e30
SQRT_HALF = 0.7071067811865476
INV_ROOT_TAU = 0.3989422804014327


def norm_forward(summed, gain, shift):
    centre = summed - jnp.mean(summed, axis=-1, keepdims=True)
    scale = lax.rsqrt(jnp.mean(centre * centre, axis=-1, keepdims=True) + NORM_EPS)
    normed = centre * scale
    return (gain * normed + shift, normed, scale)


def norm_backward(gradient, gain, normed, scale):
    scaled = gradient * gain
    centred = scaled - jnp.mean(scaled, axis=-1, keepdims=True)
    return scale * (centred - normed * jnp.mean(scaled * normed, axis=-1, keepdims=True))


def adam_update(master, first, second, gradient, rate):
    first_new = BETA_ONE * first + (1.0 - BETA_ONE) * gradient
    second_new = BETA_TWO * second + (1.0 - BETA_TWO) * gradient * gradient
    corrected = first_new / (1.0 - BETA_ONE**STEP)
    spread = jnp.sqrt(second_new / (1.0 - BETA_TWO**STEP))
    master_new = master - rate * (corrected / (spread + ADAM_EPS) + WEIGHT_DECAY * master)
    return (master_new, first_new, second_new, master_new.astype(jnp.bfloat16))


def gather_weight(shard, rows_axis):
    count = lax.axis_size("dp")
    piece = shard.shape[rows_axis] // count
    own = lax.dynamic_slice_in_dim(shard, lax.axis_index("dp") * piece, piece, rows_axis)
    return own


def mm(a, b, dims):
    return lax.dot_general(a, b, (dims, ((), ())), preferred_element_type=jnp.float32)


def per_device(
    activations,
    cotangent,
    segments,
    triple_weight,
    query_value_bias,
    output_weight,
    expand_weight,
    expand_bias,
    shrink_weight,
    vector_params,
    *state,
):
    rows, length, _ = activations.shape
    tokens = rows * length
    triple = gather_weight(triple_weight, 1)
    triple = lax.all_gather(lax.all_gather(triple, "mp", axis=2, tiled=True), "dp", axis=1, tiled=True)
    output = gather_weight(output_weight, 1)
    output = lax.all_gather(lax.all_gather(output, "mp", axis=0, tiled=True), "dp", axis=1, tiled=True)
    expand = gather_weight(expand_weight, 0)
    expand = lax.all_gather(lax.all_gather(expand, "mp", axis=1, tiled=True), "dp", axis=0, tiled=True)
    shrink = gather_weight(shrink_weight, 1)
    shrink = lax.all_gather(lax.all_gather(shrink, "mp", axis=0, tiled=True), "dp", axis=1, tiled=True)
    biases = lax.all_gather(query_value_bias, "mp", axis=1, tiled=True).reshape(2, D).astype(jnp.float32)
    expand_shift = lax.all_gather(expand_bias, "mp", axis=0, tiled=True).reshape(-1).astype(jnp.float32)
    gains = vector_params.astype(jnp.float32)
    heads = D // HEAD
    seg = lax.dynamic_slice_in_dim(segments, lax.axis_index("mp") * rows, rows, 0)
    allowed = (seg[:, :, None] == seg[:, None, :])[:, None]
    x = activations.reshape(tokens, D)
    back = cotangent.reshape(tokens, D).astype(jnp.float32)

    def split(t):
        return t.reshape(rows, length, heads, HEAD)

    query = (mm(x, triple[0], ((1,), (0,))) + biases[0]).astype(jnp.bfloat16)
    key = mm(x, triple[1], ((1,), (0,))).astype(jnp.bfloat16)
    value = (mm(x, triple[2], ((1,), (0,))) + biases[1]).astype(jnp.bfloat16)
    q4, k4, v4 = split(query), split(key), split(value)
    scores = jnp.einsum("rqhc,rkhc->rhqk", q4, k4, preferred_element_type=jnp.float32) * HEAD ** (-0.5)
    scores = jnp.where(allowed, scores, MASKED)
    row_max = jnp.max(scores, axis=-1, keepdims=True)
    weights = jnp.exp(scores - row_max)
    probs = weights / jnp.sum(weights, axis=-1, keepdims=True)
    probs_low = probs.astype(jnp.bfloat16)
    context = jnp.einsum("rhqk,rkhc->rqhc", probs_low, v4, preferred_element_type=jnp.float32)
    context = context.astype(jnp.bfloat16).reshape(tokens, D)
    attended = mm(context, output, ((1,), (0,)))
    mixed = x.astype(jnp.float32) + attended + gains[2]
    hidden, normed_one, scale_one = norm_forward(mixed, gains[0], gains[1])
    hidden_low = hidden.astype(jnp.bfloat16)
    expanded = mm(hidden_low, expand, ((1,), (0,))) + expand_shift
    cumulative = 0.5 * (1.0 + jax.scipy.special.erf(expanded * SQRT_HALF))
    active = (expanded * cumulative).astype(jnp.bfloat16)
    slope = (cumulative + expanded * jnp.exp(-0.5 * expanded * expanded) * INV_ROOT_TAU).astype(jnp.bfloat16)
    shrunk = mm(active, shrink, ((1,), (0,)))
    summed = hidden + shrunk + gains[5]
    result, normed_two, scale_two = norm_forward(summed, gains[3], gains[4])
    dsummed = norm_backward(back, gains[3], normed_two, scale_two)
    dsummed_low = dsummed.astype(jnp.bfloat16)

    def reduce_grad(part):
        part = part.astype(jnp.bfloat16)
        part = lax.psum_scatter(part, "dp", scatter_dimension=part.ndim - 2, tiled=True)
        return lax.psum_scatter(part, "mp", scatter_dimension=part.ndim - 1, tiled=True).astype(jnp.float32)

    shrink_grad = reduce_grad(mm(dsummed_low, active, ((0,), (0,))))
    dactive = mm(dsummed_low, shrink, ((1,), (1,)))
    dexpanded = (dactive * slope).astype(jnp.bfloat16)
    expand_grad = reduce_grad(mm(hidden_low, dexpanded, ((0,), (0,))))
    dhidden = dsummed + mm(dexpanded, expand, ((1,), (1,)))
    dmixed = norm_backward(dhidden, gains[0], normed_one, scale_one)
    dmixed_low = dmixed.astype(jnp.bfloat16)
    output_grad = reduce_grad(mm(dmixed_low, context, ((0,), (0,))))
    dcontext = split(mm(dmixed_low, output, ((1,), (1,))).astype(jnp.bfloat16))
    dvalue = jnp.einsum("rhqk,rqhc->rkhc", probs_low, dcontext, preferred_element_type=jnp.float32)
    dprobs = jnp.einsum("rqhc,rkhc->rhqk", dcontext, v4, preferred_element_type=jnp.float32)
    inner = jnp.sum(probs * dprobs, axis=-1, keepdims=True)
    dscores = (probs * (dprobs - inner)).astype(jnp.bfloat16)
    dquery = jnp.einsum("rhqk,rkhc->rqhc", dscores, k4, preferred_element_type=jnp.float32) * HEAD ** (-0.5)
    dkey = jnp.einsum("rhqk,rqhc->rkhc", dscores, q4, preferred_element_type=jnp.float32) * HEAD ** (-0.5)
    dthree = [t.astype(jnp.bfloat16).reshape(tokens, D) for t in (dquery, dkey, dvalue)]
    triple_grad = reduce_grad(jnp.stack([mm(x, t, ((0,), (0,))) for t in dthree]))
    input_grad = dmixed
    for j in range(3):
        input_grad = input_grad + mm(dthree[j], triple[j], ((1,), (1,)))

    def total(t):
        return jnp.sum(t.astype(jnp.float32), axis=0)

    vector_grad = jnp.stack([
        total(dhidden * normed_one), total(dhidden), total(dmixed),
        total(back * normed_two), total(back), total(dsummed),
        total(dthree[0]), total(dthree[2]),
    ])
    vector_grad = lax.psum(jnp.concatenate([vector_grad, total(dexpanded).reshape(4, D)]), ("dp", "mp"))
    dp, mp = lax.axis_index("dp"), lax.axis_index("mp")
    groups, parts = lax.axis_size("mp"), lax.axis_size("dp")
    width = D // (groups * parts)
    vec = lax.dynamic_slice_in_dim(vector_grad[:6], (dp * groups + mp) * width, width, 1)
    qv = vector_grad[6:8].reshape(2, heads, HEAD)
    qv = lax.dynamic_slice_in_dim(qv, mp * (heads // groups), heads // groups, 1)
    qv = lax.dynamic_slice_in_dim(qv, dp * (HEAD // parts), HEAD // parts, 2)
    eb = vector_grad[8:].reshape(FF // HEAD, HEAD)
    eb = lax.dynamic_slice_in_dim(eb, mp * (FF // HEAD // groups), FF // HEAD // groups, 0)
    eb = lax.dynamic_slice_in_dim(eb, dp * (HEAD // parts), HEAD // parts, 1)
    grads = (triple_grad, qv, output_grad.T, expand_grad, eb, shrink_grad.T, vec)
    rates = (D ** (-0.5), 0.5, (D // 16) ** (-0.5), D ** (-0.5), 0.5, FF ** (-0.5), 0.3)
    outs = (result.astype(jnp.bfloat16).reshape(activations.shape), input_grad.reshape(activations.shape))
    for i in range(7):
        outs = outs + adam_update(state[3 * i], state[3 * i + 1], state[3 * i + 2], grads[i], rates[i])
    return outs


STATE_SPECS = (
    P(None, "dp", "mp"),
    P(None, "mp", "dp"),
    P("mp", "dp"),
    P("dp", "mp"),
    P("mp", "dp"),
    P("mp", "dp"),
    P(None, ("dp", "mp")),
)


def solution(mesh):
    rows = P(("dp", "mp"), None, None)
    placed = (
        rows,
        rows,
        P("dp", None),
        P(None, None, "mp"),
        P(None, "mp", None),
        P("mp", None),
        P(None, "mp"),
        P("mp", None),
        P("mp", None),
        P(),
    )
    for spec in STATE_SPECS:
        placed = placed + (spec,) * 3
    out_specs = (rows, rows)
    for spec in STATE_SPECS:
        out_specs = out_specs + (spec,) * 4
    return jax.shard_map(per_device, mesh=mesh, in_specs=placed, out_specs=out_specs, check_vma=False)
```

time: 1540 us -> 657 us (0.43)
  waiting for transfers between devices: 1060 us -> 142 us
  blocking collectives: 62.8 us -> 133 us
  other arithmetic: 88 us -> 61.6 us
  local copies, waits for them, and re-layouts: 85.2 us -> 109 us
  matrix products: 212 us -> 189 us
    all_gather x16 -> x4, waiting for transfers between devices: 501 us -> 0.05 us  [the longest x1 0.02 us: per_device(): lax.all_gather(lax.all_gather(expand, 'mp', axis=1, tiled=True), 'dp', ax...]
    reduce_scatter x18 -> x6, waiting for transfers between devices: 557 us -> 104 us  [the longest x3 56.5 us: reduce_grad(): lax.psum_scatter(part, 'mp', scatter_dimension=part.ndim - 1, tiled=True)]
    all_gather x0 -> x6, blocking collectives: none -> 93.6 us  [the longest x1 21.7 us: per_device(): lax.all_gather(triple, 'mp', axis=2, tiled=True)]
    unnamed x2 -> x0, blocking collectives: 62.8 us -> none
    reshape x2 -> x12, local copies, waits for them, and re-layouts: 0.09 us -> 45.4 us  [the longest x5 27.2 us: split(): return t.reshape(rows, length, heads, HEAD)]
    psum x0 -> x1, blocking collectives: none -> 39.7 us  [per_device(): lax.psum(jnp.concatenate([vector_grad, total(dexpanded).reshape(4, D)]),...]
    unnamed x38 -> x14, waiting for transfers between devices: 4.48 us -> 37.4 us
    reduce_sum x18 -> x4, other arithmetic: 35 us -> 8.38 us  [total(): return jnp.sum(t.astype(jnp.float32), axis=0)]
  transfers between devices with their start and end apart: 36 -> 12, of which waited for: 32 -> 7; matrix products, arithmetic and copies ran while one was open for 19% -> 36% of each run, Pallas kernels for 0% -> 0%
where the time goes in v1:
time: 657 us; the launch traced here: 650 us
  matrix products  189 us (29%)
  waiting for transfers between devices  142 us (22%)
  blocking collectives  133 us (20%)
  local copies, waits for them, and re-layouts  109 us (17%)
  other arithmetic  61.6 us (9%)
  between operations  15.1 us (2%)
    dot_general x18, matrix products, mm(): lax.dot_general(a, b, (dims, ((), ())), preferred_element_type=jnp.float32)  123 us
    reduce_scatter x3, waiting for transfers between devices, reduce_grad(): lax.psum_scatter(part, 'mp', scatter_dimension=part.ndim - 1, tiled=True)  56.5 us
    reduce_scatter x3, waiting for transfers between devices, reduce_grad(): lax.psum_scatter(part, 'dp', scatter_dimension=part.ndim - 2, tiled=True)  48 us
    unnamed x109, local copies, waits for them, and re-layouts  41.8 us
    psum x1, blocking collectives, per_device(): lax.psum(jnp.concatenate([vector_grad, total(dexpanded).reshape(4, D)]),...  39.7 us
    unnamed x14, waiting for transfers between devices  37.4 us
    reshape x5, local copies, waits for them, and re-layouts, split(): return t.reshape(rows, length, heads, HEAD)  27.2 us
    sub x1, other arithmetic, per_device(): weights = jnp.exp(scores - row_max)  25.5 us
  transfers between devices with their start and end apart: 12, of which 7 were waited for; matrix products, arithmetic and copies ran while one was open for 36% of the time, Pallas kernels for 0%

profile of v1, /device:TPU:0, one launch (start us, length us, event | category | flops | bytes accessed | tf_op | source)
XLA Modules:
  0.0 650.5 jit_solution(2121431900021771325)
XLA Ops:
  8.6 21.7 %all_gather.30 = bf16[3,96,768]{1,0,2:T(4,128)(2,1)} all-gather(bf16[3,96,192]{1,0,2:T(4,128)(2,1)S(1)} %copy.234), channel_id=1, replica_groups=mesh['dp'=8,'mp'=4] {'mp'}, dimensions={2}, use_global_device_ids=true | all-gather | bytes 552960 | tf_op jit(solution)/shard_map/all_gather | solution.py:71
  30.3 2.2 copy.179
  33.6 13.6 %all_gather.33 = bf16[768,96]{1,0:T(8,128)(2,1)S(1)} all-gather(bf16[192,96]{1,0:T(8,128)(2,1)S(1)} %constant_dynamic-slice_fusion.2), channel_id=1, replica_groups=mesh['dp'=8,'mp'=4] {'mp'}, dimensions={0}, use_global_device_ids=true | all-gather | bytes 184320 | tf_op jit(solution)/shard_map/all_gather | solution.py:73
  48.1 17.4 %all_gather.35 = bf16[96,3072]{1,0:T(8,128)(2,1)} all-gather(bf16[96,768]{1,0:T(8,128)(2,1)S(1)} %constant_dynamic-slice_fusion.1), channel_id=1, replica_groups=mesh['dp'=8,'mp'=4] {'mp'}, dimensions={1}, use_global_device_ids=true | all-gather | bytes 737280 | tf_op jit(solution)/shard_map/all_gather | solution.py:75
  66.9 15.8 %all_gather.38 = bf16[3072,96]{0,1:T(8,128)(2,1)} all-gather(bf16[768,96]{0,1:T(8,128)(2,1)S(1)} %copy.235), channel_id=1, replica_groups=mesh['dp'=8,'mp'=4] {'mp'}, dimensions={0}, use_global_device_ids=true | all-gather | bytes 737280 | tf_op jit(solution)/shard_map/all_gather | solution.py:77
  82.8 11.9 %all_gather.32 = bf16[2,12,64]{2,0,1:T(2,128)(2,1)S(1)} all-gather(bf16[2,3,64]{2,0,1:T(2,128)(2,1)S(1)} %copy-done.35), channel_id=1, replica_groups=mesh['dp'=8,'mp'=4] {'mp'}, dimensions={1}, use_global_device_ids=true | all-gather | bytes 3840 | tf_op jit(solution)/shard_map/all_gather | solution.py:78
  96.0 13.1 %all-gather = bf16[4,12,64]{2,1,0:T(8,128)(2,1)S(1)} all-gather(bf16[1,12,64]{2,1,0:T(8,128)(2,1)S(1)} %bitcast.132), channel_id=1, replica_groups=mesh['dp'=8,'mp'=4] {'mp'}, dimensions={0}, use_global_device_ids=true | all-gather | bytes 7680 | tf_op jit(solution)/shard_map/all_gather | solution.py:79
  110.8 4.9 fusion.27
  115.7 5.1 reshape.182
  120.9 5.6 fusion.29
  126.5 5.7 reshape.183
  132.2 5.0 fusion.28
  137.2 5.6 reshape.181
  142.8 11.8 %fusion.36 = f32[4,12,288,288]{2,3,1,0:T(8,128)} fusion(bf16[4,288,12,64]{1,0,3,2:T(4,128)(2,1)} %reshape.183, bf16[4,288,12,64]{1,0,3,2:T(4,128)(2,1)S(1)} %reshape.182), kind=kOutput, calls=%fused_computation.80 | convolution fusion | flops 509607936 | bytes 19464192 | tf_op jit(solution)/shard_map/rqhc,rkhc->rhqk/dot_general | solution.py:94
  154.6 25.5 %fusion.85 = (f32[4,12,288]{2,1,0:T(8,128)S(1)}, f32[4,12,288,288]{2,3,1,0:T(8,128)}) fusion(f32[4,12,288,288]{2,3,1,0:T(8,128)} %fusion.36, pred[4,288,288]{1,2,0:T(8,128)(4,1)S(1)} %broadcast_compare_fusion), kind=kOutput, calls=%fused_computation.169 | output fusion | flops 23888160 | bytes 32237568 | tf_op jit(solution)/shard_map/sub | solution.py:97
  180.1 9.3 %convert_bitcast_fusion.1 = bf16[4,288,12,64]{1,3,2,0:T(8,128)(2,1)S(1)} fusion(bf16[4,288,12,64]{1,0,3,2:T(4,128)(2,1)S(1)} %copy-done.15, f32[4,12,288,288]{2,3,1,0:T(8,128)} %get-tuple-element.200, f32[4,12,288]{2,1,0:T(8,128)S(1)} %get-tuple-element.199), kind=kOutput, calls=%fused_computation.75 | convolution fusion | flops 518455296 | bytes 19519488 | tf_op jit(solution)/shard_map/rhqk,rkhc->rqhc/dot_general | solution.py:100
  189.4 1.8 copy.184
  191.2 2.7 reshape.184
  193.9 4.2 fusion.86
  198.2 1.8 copy-done.9
  200.6 13.7 %multiply_convert_fusion.1 = (bf16[1152,3072]{1,0:T(8,128)(2,1)}, f32[1152,3072]{1,0:T(8,128)}) fusion(f32[3072]{0:T(1024)S(1)} %reshape.194, bf16[768,3072]{1,0:T(8,128)(2,1)} %all-gather.10.cloned.1.call-done, f32[1152,768]{1,0:T(8,128)} %copy-done.9, f32[768]{0:T(1024)S(1)} %get-tuple-element.161, f32[1152]{0:T(1024)S(1)} %add_rsqrt_fusion.1, ...), kind=kOutput, calls=%fused_computation.14 | convolution fusion | flops 5461475328 | bytes 29518848 | tf_op jit(solution)/shard_map/dot_general | solution.py:52
  214.3 11.8 %fusion.87 = (f32[1152]{0:T(1024)S(1)}, f32[1152,768]{1,0:T(8,128)S(1)}) fusion(f32[768]{0:T(1024)S(1)} %get-tuple-element.160, bf16[1152,3072]{1,0:T(8,128)(2,1)} %get-tuple-element.203, bf16[3072,768]{0,1:T(8,128)(2,1)} %all-gather.12.cloned.1.call-done, f32[768]{0:T(1024)S(1)} %get-tuple-element.161, f32[1152]{0:T(1024)S(1)} %add_rsqrt_fusion.1, ...), kind=kOutput, calls=%fused_computation.171 | convolution fusion | flops 5442010112 | bytes 18897408 | tf_op jit(solution)/shard_map/dot_general | solution.py:52
  227.5 1.9 fusion.23
  229.5 3.1 fusion.81
  232.6 16.6 %convert_reduce_fusion = (f32[3072]{0:T(1024)}, bf16[1152,3072]{1,0:T(8,128)(2,1)}) fusion(f32[1152,3072]{1,0:T(8,128)} %get-tuple-element.204, bf16[3072,768]{0,1:T(8,128)(2,1)S(1)} %copy-done.36, f32[1152,768]{1,0:T(8,128)S(1)} %get-tuple-element.184), kind=kOutput, calls=%fused_computation.13 | convolution fusion | flops 5486244864 | bytes 29503488 | tf_op jit(solution)/shard_map/dot_general | solution.py:52
  249.2 9.7 %multiply_reduce_fusion.1 = (f32[768]{0:T(1024)}, f32[1152]{0:T(1024)S(1)}, f32[1152]{0:T(1024)S(1)}, f32[768]{0:T(1024)}, f32[1152,768]{1,0:T(8,128)S(1)}) fusion(f32[1152,768]{1,0:T(8,128)S(1)} %copy-done.10, f32[1152]{0:T(1024)S(1)} %add_rsqrt_fusion.1, f32[1152]{0:T(1024)S(1)} %broadcast_multiply_fusion.4, f32[768]{0:T(1024)S(1)} %get-tuple-element.163, ...), kind=kOutput, calls=%fused_computation.54 | convolution fusion | flops 5444661248 | bytes 22440960 | tf_op jit(solution)/shard_map/dot_general | solution.py:52
  258.9 1.8 fusion.83
  260.7 1.8 copy-done.12
  264.1 4.7 reshape.204
  268.7 6.1 copy.188
  274.9 12.8 %convert_reduce_fusion.1 = (f32[12,64]{1,0:T(8,128)}, bf16[4,288,12,64]{1,3,2,0:T(8,128)(2,1)}) fusion(bf16[4,288,12,64]{1,3,2,0:T(8,128)(2,1)S(1)} %copy.188, f32[4,12,288,288]{2,3,1,0:T(8,128)} %get-tuple-element.200, f32[4,12,288]{2,1,0:T(8,128)S(1)} %get-tuple-element.199), kind=kOutput, calls=%fused_computation.28 | convolution fusion | flops 520224000 | bytes 19522560 | tf_op jit(solution)/shard_map/rhqk,rqhc->rkhc/dot_general | solution.py:130
  287.7 18.2 %multiply_reduce_fusion = (f32[4,12,288]{2,1,0:T(8,128)S(1)}, f32[4,12,288,288]{2,3,1,0:T(8,128)}) fusion(f32[4,12,288,288]{2,3,1,0:T(8,128)} %get-tuple-element.200, f32[4,12,288]{2,1,0:T(8,128)S(1)} %get-tuple-element.199, bf16[4,288,12,64]{1,3,2,0:T(8,128)(2,1)S(1)} %copy.188, bf16[4,288,12,64]{1,0,3,2:T(4,128)(2,1)} %reshape.181), kind=kOutput, calls=%fused_computation.2 | convolution fusion | flops 521538048 | bytes 35500032 | tf_op jit(solution)/shard_map/rqhc,rkhc->rhqk/dot_general | solution.py:131
  305.9 5.3 convolution_convert_fusion.4
  311.2 14.6 %multiply_convert_fusion = bf16[4,12,288,288]{2,3,1,0:T(8,128)(2,1)S(1)} fusion(f32[4,12,288,288]{2,3,1,0:T(8,128)} %get-tuple-element.209, f32[4,12,288]{2,1,0:T(8,128)S(1)} %get-tuple-element.208, f32[4,12,288,288]{2,3,1,0:T(8,128)} %get-tuple-element.200, f32[4,12,288]{2,1,0:T(8,128)S(1)} %get-tuple-element.199), kind=kLoop, calls=%fused_computation.1 | loop fusion | flops 15925248 | bytes 39923712 | tf_op jit(solution)/shard_map/convert_element_type | solution.py:133
  325.8 4.0 copy-done.2
  329.8 3.6 convert_reduce_fusion.2
  333.5 9.4 %fusion.31 = bf16[4,288,12,64]{1,3,2,0:T(8,128)(2,1)} fusion(bf16[4,12,288,288]{2,3,1,0:T(8,128)(2,1)} %copy-done.2, bf16[4,288,12,64]{1,0,3,2:T(4,128)(2,1)S(1)} %copy-done.4), kind=kOutput, calls=%fused_computation.73 | convolution fusion | flops 511377408 | bytes 11501568 | tf_op jit(solution)/shard_map/rhqk,rqhc->rkhc/dot_general | solution.py:135
  342.9 3.2 copy.198
  346.1 5.0 reshape.189
  351.2 3.2 copy.195
  354.4 4.8 reshape.188
  359.2 3.2 copy.192
  362.5 4.8 reshape.187
  367.3 3.3 fusion.48
  372.4 1.7 fusion.46
  374.1 2.0 pad_maximum_fusion
  376.1 8.1 %copy.228 = bf16[3,768,768]{2,0,1:T(4,128)(2,1)} copy(bf16[3,768,768]{1,2,0:T(8,128)(2,1)} %pad_maximum_fusion) | data formatting | bytes 7077888
  384.2 4.9 copy.237
  389.8 12.2 %convolution_convert_fusion.1 = bf16[768,3072]{1,0:T(8,128)(2,1)} fusion(bf16[1152,3072]{1,0:T(8,128)(2,1)} %get-tuple-element.215, f32[1152,768]{1,0:T(8,128)} %copy-done.9, f32[768]{0:T(1024)S(1)} %copy-done.34, f32[1152]{0:T(1024)S(1)} %copy-done.25, f32[1152]{0:T(1024)S(1)} %broadcast_multiply_fusion.4, f32[768]{0:T(1024)S(1)} %copy-done.30), kind=kOutput, calls=%fused_computation.27 | convolution fusion | flops 5442600960 | bytes 15350784 | tf_op jit(solution)/shard_map/dot_general | solution.py:52
  402.1 11.1 %convolution_convert_fusion = bf16[768,3072]{1,0:T(8,128)(2,1)} fusion(bf16[1152,3072]{1,0:T(8,128)(2,1)} %get-tuple-element.203, f32[1152,768]{1,0:T(8,128)} %copy-done.13), kind=kOutput, calls=%fused_computation.26 | convolution fusion | flops 5439062016 | bytes 15335424 | tf_op jit(solution)/shard_map/dot_general | solution.py:52
  413.3 1.8 copy.230
  415.2 20.6 %reduce-scatter.25.cloned.1.call-done = bf16[96,2304]{1,0:T(8,128)(2,1)} async-done(((bf16[768,2304]{1,0:T(8,128)(2,1)}), bf16[96,2304]{1,0:T(8,128)(2,1)}) %reduce-scatter.25.cloned.1.call-update) | async-done | bytes 442384
  439.1 1.8 copy.202
  447.6 39.7 %psum.7 = f32[12,768]{1,0:T(8,128)S(1)} all-reduce(f32[12,768]{1,0:T(8,128)S(1)} %concatenate.3), channel_id=1, replica_groups=mesh['dp'=8,'mp'=4] {'dp','mp'}, use_global_device_ids=true, to_apply=%region_22.23 | all-reduce | flops 9216 | bytes 73728 | tf_op jit(solution)/shard_map/psum | solution.py:150
  495.5 4.6 convolution_add_fusion.5
  500.2 4.7 convolution_add_fusion.4
  504.9 46.3 %reduce-scatter.21.cloned.1.call-done = bf16[96,3072]{1,0:T(8,128)(2,1)} async-done(((bf16[768,3072]{1,0:T(8,128)(2,1)}), bf16[96,3072]{1,0:T(8,128)(2,1)}) %reduce-scatter.21.cloned.1.call-update) | async-done | bytes 589840 | tf_op jit(solution)/shard_map/reduce_scatter | solution.py:118
  551.3 5.7 convolution_add_fusion.3
  557.0 16.5 %reduce-scatter.27.cloned.1.call-done = bf16[192,96]{1,0:T(8,128)(2,1)} async-done(((bf16[768,96]{1,0:T(8,128)(2,1)}), bf16[192,96]{1,0:T(8,128)(2,1)}) %reduce-scatter.27.cloned.1.call-update) | async-done | bytes 36880
  577.5 18.4 %reduce-scatter.13.cloned.1.call-done = bf16[3,96,192]{1,2,0:T(8,128)(2,1)} async-done(((bf16[3,96,768]{1,2,0:T(8,128)(2,1)}), bf16[3,96,192]{1,2,0:T(8,128)(2,1)}) %reduce-scatter.13.cloned.1.call-update) | async-done | bytes 110608 | tf_op jit(solution)/shard_map/reduce_scatter | solution.py:119
  600.6 17.9 %reduce-scatter.19.cloned.1.call-done = bf16[96,768]{1,0:T(8,128)(2,1)} async-done(((bf16[96,3072]{1,0:T(8,128)(2,1)}), bf16[96,768]{1,0:T(8,128)(2,1)}) %reduce-scatter.19.cloned.1.call-update) | async-done | bytes 147472 | tf_op jit(solution)/shard_map/reduce_scatter | solution.py:119
  618.5 2.2 fusion.76
  620.8 20.3 %reduce-scatter.23.cloned.1.call-done = bf16[96,768]{1,0:T(8,128)(2,1)} async-done(((bf16[96,3072]{1,0:T(8,128)(2,1)}), bf16[96,768]{1,0:T(8,128)(2,1)}) %reduce-scatter.23.cloned.1.call-update) | async-done | bytes 147472 | tf_op jit(solution)/shard_map/reduce_scatter | solution.py:119
  641.0 2.4 fusion.72
  (181 shorter events, 40.7 us)
Async XLA Ops:
  7.2 40.9 %copy-start = (bf16[768,768]{1,0:T(8,128)(2,1)S(1)}, bf16[768,768]{1,0:T(8,128)(2,1)}, u32[]{:S(2)}) copy-start(bf16[768,768]{1,0:T(8,128)(2,1)} %param.37) | copy-start | bytes 3538948
  7.2 103.6 %all-gather.6.cloned.1.call-start = ((), (), s32[]{:S(2)}) async-start(), calls=%async_computation.8 | async-start | bytes 3981312 | tf_op jit(solution)/shard_map/all_gather | solution.py:71
  8.6 74.2 %copy-start.35 = (bf16[2,3,64]{2,0,1:T(2,128)(2,1)S(1)}, bf16[2,3,64]{2,0,1:T(2,128)(2,1)}, u32[]{:S(2)}) copy-start(bf16[2,3,64]{2,0,1:T(2,128)(2,1)} %param.35) | copy-start | bytes 2308
  30.3 65.6 %copy-start.31 = (bf16[6,768]{1,0:T(8,128)(2,1)S(1)}, bf16[6,768]{1,0:T(8,128)(2,1)}, u32[]{:S(2)}) copy-start(bf16[6,768]{1,0:T(8,128)(2,1)} %param.40) | copy-start | bytes 27652
  30.3 65.7 %copy-start.32 = (bf16[12,64]{1,0:T(8,128)(2,1)S(1)}, bf16[12,64]{1,0:T(8,128)(2,1)}, u32[]{:S(2)}) copy-start(bf16[12,64]{1,0:T(8,128)(2,1)} %param.38) | copy-start | bytes 4612
  30.3 78.9 %copy-start.6 = (bf16[4,288,768]{2,1,0:T(8,128)(2,1)S(1)}, bf16[4,288,768]{2,1,0:T(8,128)(2,1)}, u32[]{:S(2)}) copy-start(bf16[4,288,768]{2,1,0:T(8,128)(2,1)} %param.32) | copy-start | bytes 5308420
  32.6 161.4 %all-gather.8.cloned.1.call-start = ((), (), s32[]{:S(2)}) async-start(), calls=%async_computation.9 | async-start | bytes 1327104 | tf_op jit(solution)/shard_map/all_gather | solution.py:73
  48.0 152.5 %all-gather.10.cloned.1.call-start = ((), (), s32[]{:S(2)}) async-start(), calls=%async_computation.10 | async-start | bytes 5308416 | tf_op jit(solution)/shard_map/all_gather | solution.py:75
  65.6 148.7 %all-gather.12.cloned.1.call-start = ((), (), s32[]{:S(2)}) async-start(), calls=%async_computation.11 | async-start | bytes 5308416 | tf_op jit(solution)/shard_map/all_gather | solution.py:77
  82.7 330.6 %reduce-scatter.15.cloned.1.call-start = ((), (), s32[]{:S(2)}) async-start(), calls=%async_computation.13 | async-start | bytes 1327104 | tf_op jit(solution)/shard_map/reduce_scatter | solution.py:118
  95.9 118.3 %copy-start.33 = (f32[768]{0:T(1024)}, f32[768]{0:T(1024)S(1)}, u32[]{:S(2)}) copy-start(f32[768]{0:T(1024)S(1)} %get-tuple-element.161) | copy-start | bytes 9220
  96.0 162.9 %copy-start.29 = (f32[768]{0:T(1024)}, f32[768]{0:T(1024)S(1)}, u32[]{:S(2)}) copy-start(f32[768]{0:T(1024)S(1)} %get-tuple-element.163) | copy-start | bytes 9220
  120.8 22.0 %copy-start.3 = (bf16[4,288,12,64]{1,0,3,2:T(4,128)(2,1)}, bf16[4,288,12,64]{1,0,3,2:T(4,128)(2,1)S(1)}, u32[]{:S(2)}) copy-start(bf16[4,288,12,64]{1,0,3,2:T(4,128)(2,1)S(1)} %reshape.182) | copy-start | bytes 5308420
  154.6 25.5 %copy-start.15 = (bf16[4,288,12,64]{1,0,3,2:T(4,128)(2,1)S(1)}, bf16[4,288,12,64]{1,0,3,2:T(4,128)(2,1)}, u32[]{:S(2)}) copy-start(bf16[4,288,12,64]{1,0,3,2:T(4,128)(2,1)} %reshape.181) | copy-start | bytes 5308420
  198.1 1.8 copy-start.9
  200.5 58.4 %copy-start.24 = (f32[1152]{0:T(1024)}, f32[1152]{0:T(1024)S(1)}, u32[]{:S(2)}) copy-start(f32[1152]{0:T(1024)S(1)} %add_rsqrt_fusion.1) | copy-start | bytes 13828
  226.1 1.5 copy-start.7
  229.5 3.1 copy-start.36
  229.5 19.7 %slice-start = ((s8[4718592]{0:T(1024)(128)(4,1)}), s8[4194304]{0:T(1024)(128)(4,1)S(1)}, s32[]{:S(2)}) async-start(s8[4718592]{0:T(1024)(128)(4,1)} %bitcast.133), calls=%async_computation.20 | async-start | bytes 8388608
  232.5 16.7 %copy-start.13 = (f32[1152,768]{1,0:T(8,128)}, f32[1152,768]{1,0:T(8,128)S(1)}, u32[]{:S(2)}) copy-start(f32[1152,768]{1,0:T(8,128)S(1)} %get-tuple-element.184) | copy-start | bytes 10616836
  232.5 16.7 %copy-start.10 = (f32[1152,768]{1,0:T(8,128)S(1)}, f32[1152,768]{1,0:T(8,128)}, u32[]{:S(2)}) copy-start(f32[1152,768]{1,0:T(8,128)} %copy-done.9) | copy-start | bytes 10616836
  232.6 16.7 %slice-start.1 = ((s8[4718592]{0:T(1024)(128)(4,1)}), s8[524288]{0:T(1024)(128)(4,1)S(1)}, s32[]{:S(2)}) async-start(s8[4718592]{0:T(1024)(128)(4,1)} %bitcast.133), calls=%async_computation.21 | async-start | bytes 1048576
  258.9 3.6 copy-start.38
  260.7 1.8 copy-start.12
  311.2 18.6 %copy-start.5 = (bf16[4,288,12,64]{1,0,3,2:T(4,128)(2,1)S(1)}, bf16[4,288,12,64]{1,0,3,2:T(4,128)(2,1)}, u32[]{:S(2)}) copy-start(bf16[4,288,12,64]{1,0,3,2:T(4,128)(2,1)} %reshape.183) | copy-start | bytes 5308420
  325.8 4.0 copy-start.2
  329.8 3.7 copy-start.4
  333.5 102.4 %reduce-scatter.25.cloned.1.call-start = ((), (), s32[]{:S(2)}) async-start(), calls=%async_computation.18 | async-start | bytes 3981312
  333.5 9.4 %copy-start.14 = (bf16[4,288,12,64]{1,3,2,0:T(8,128)(2,1)S(1)}, bf16[4,288,12,64]{1,3,2,0:T(8,128)(2,1)}, u32[]{:S(2)}) copy-start(bf16[4,288,12,64]{1,3,2,0:T(8,128)(2,1)} %get-tuple-element.213) | copy-start | bytes 5308420
  342.9 8.3 %copy-start.8 = (bf16[4,288,12,64]{1,3,2,0:T(8,128)(2,1)S(1)}, bf16[4,288,12,64]{1,3,2,0:T(8,128)(2,1)}, u32[]{:S(2)}) copy-start(bf16[4,288,12,64]{1,3,2,0:T(8,128)(2,1)} %fusion.31) | copy-start | bytes 5308420
  354.4 4.8 copy-start.11
  362.5 4.8 copy-start.16
  367.3 3.4 copy-start.17
  367.3 3.4 copy-start.37
  370.7 1.7 copy-start.19
  389.1 0.7 copy-start.25
  389.1 0.7 copy-start.30
  389.1 0.7 copy-start.34
  389.1 104.7 %reduce-scatter.17.cloned.1.call-start = ((), (), s32[]{:S(2)}) async-start(), calls=%async_computation.14 | async-start | bytes 5308416 | tf_op jit(solution)/shard_map/reduce_scatter | solution.py:118
  402.0 149.2 %reduce-scatter.21.cloned.1.call-start = ((), (), s32[]{:S(2)}) async-start(), calls=%async_computation.16 | async-start | bytes 5308416 | tf_op jit(solution)/shard_map/reduce_scatter | solution.py:118
  413.2 25.6 %copy-start.26 = (f32[768]{0:T(1024)S(1)}, f32[768]{0:T(1024)}, u32[]{:S(2)}) copy-start(f32[768]{0:T(1024)} %get-tuple-element.156) | copy-start | bytes 9220
  413.2 25.6 %copy-start.20 = (f32[3,96,192]{2,1,0:T(8,128)S(1)}, f32[3,96,192]{2,1,0:T(8,128)}, u32[]{:S(2)}) copy-start(f32[3,96,192]{2,1,0:T(8,128)} %param.42) | copy-start | bytes 663556
  413.2 25.7 %copy-start.21 = (f32[3,96,192]{2,1,0:T(8,128)S(1)}, f32[3,96,192]{2,1,0:T(8,128)}, u32[]{:S(2)}) copy-start(f32[3,96,192]{2,1,0:T(8,128)} %param.43) | copy-start | bytes 663556
  413.2 31.5 %copy-start.28 = (f32[768]{0:T(1024)S(1)}, f32[768]{0:T(1024)}, u32[]{:S(2)}) copy-start(f32[768]{0:T(1024)} %get-tuple-element.185) | copy-start | bytes 9220
  413.2 33.6 %copy-start.27 = (f32[768]{0:T(1024)S(1)}, f32[768]{0:T(1024)}, u32[]{:S(2)}) copy-start(f32[768]{0:T(1024)} %get-tuple-element.183) | copy-start | bytes 9220
  413.2 160.3 %reduce-scatter.27.cloned.1.call-start = ((), (), s32[]{:S(2)}) async-start(), calls=%async_computation.19 | async-start | bytes 245760
  415.2 180.7 %reduce-scatter.13.cloned.1.call-start = ((), (), s32[]{:S(2)}) async-start(), calls=%async_computation.12 | async-start | bytes 737280 | tf_op jit(solution)/shard_map/reduce_scatter | solution.py:119
  438.7 179.8 %reduce-scatter.19.cloned.1.call-start = ((), (), s32[]{:S(2)}) async-start(), calls=%async_computation.15 | async-start | bytes 737280 | tf_op jit(solution)/shard_map/reduce_scatter | solution.py:119
  493.9 147.2 %reduce-scatter.23.cloned.1.call-start = ((), (), s32[]{:S(2)}) async-start(), calls=%async_computation.17 | async-start | bytes 737280 | tf_op jit(solution)/shard_map/reduce_scatter | solution.py:119
  495.5 4.7 copy-start.18
  557.0 61.5 %copy-start.22 = (f32[96,768]{1,0:T(8,128)S(1)}, f32[96,768]{1,0:T(8,128)}, u32[]{:S(2)}) copy-start(f32[96,768]{1,0:T(8,128)} %param.50) | copy-start | bytes 884740
  557.0 61.5 %copy-start.23 = (f32[96,768]{1,0:T(8,128)S(1)}, f32[96,768]{1,0:T(8,128)}, u32[]{:S(2)}) copy-start(f32[96,768]{1,0:T(8,128)} %param.51) | copy-start | bytes 884740
  595.9 47.6 %copy-start.1 = (bf16[768,768]{1,0:T(8,128)(2,1)S(1)}, bf16[768,768]{1,0:T(8,128)(2,1)}, u32[]{:S(2)}) copy-start(bf16[768,768]{1,0:T(8,128)(2,1)} %param.37) | copy-start | bytes 3538948
Sparse Core Ops, SparseCore 0:
  32.7 33.7 all-gather.5
  68.9 24.0 all-gather.7
  94.9 38.9 all-gather.9
  135.6 38.9 all-gather.11
  333.6 35.1 reduce-scatter.14
  389.3 46.5 reduce-scatter.24
  439.7 54.1 reduce-scatter.16
  497.3 53.9 reduce-scatter.20
  554.2 19.3 reduce-scatter.26
  575.7 20.1 reduce-scatter.12
  598.1 20.3 reduce-scatter.18
  620.7 20.3 reduce-scatter.22

commit v2 on v1

v2 whole, which is shorter than its diff:
```python
import jax
import jax.numpy as jnp
from jax import lax
from jax.experimental import pallas as pl
from jax.experimental.pallas import tpu as pltpu
from jax.sharding import PartitionSpec as P

D = 768
HEAD = 64
FF = 3072
STEP = 10


NORM_EPS = 1e-05
BETA_ONE = 0.5
BETA_TWO = 0.6
ADAM_EPS = 1e-08
WEIGHT_DECAY = 0.01
MASKED = -1e30
SQRT_HALF = 0.7071067811865476
INV_ROOT_TAU = 0.3989422804014327


def norm_forward(summed, gain, shift):
    centre = summed - jnp.mean(summed, axis=-1, keepdims=True)
    scale = lax.rsqrt(jnp.mean(centre * centre, axis=-1, keepdims=True) + NORM_EPS)
    normed = centre * scale
    return (gain * normed + shift, normed, scale)


def norm_backward(gradient, gain, normed, scale):
    scaled = gradient * gain
    centred = scaled - jnp.mean(scaled, axis=-1, keepdims=True)
    return scale * (centred - normed * jnp.mean(scaled * normed, axis=-1, keepdims=True))


def adam_update(master, first, second, gradient, rate):
    first_new = BETA_ONE * first + (1.0 - BETA_ONE) * gradient
    second_new = BETA_TWO * second + (1.0 - BETA_TWO) * gradient * gradient
    corrected = first_new / (1.0 - BETA_ONE**STEP)
    spread = jnp.sqrt(second_new / (1.0 - BETA_TWO**STEP))
    master_new = master - rate * (corrected / (spread + ADAM_EPS) + WEIGHT_DECAY * master)
    return (master_new, first_new, second_new, master_new.astype(jnp.bfloat16))


MESH = pl.DeviceIdType.MESH
BF = jnp.bfloat16
F32 = jnp.float32
HALF = 48
SLICE = 96
SMALL = 16


def place():
    p, z = lax.axis_index("dp"), lax.axis_index("mp")
    core, xy = p % 2, p // 2
    x, y = xy % 2, xy // 2
    return p, z, core, xy, p + 1 - 2 * core, p + 2 - 4 * x, p + 4 - 8 * y, xy + 1 - 2 * x, xy + 2 - 4 * y


def remote(src, dst, send_sem, recv_sem, p, z):
    return pltpu.make_async_remote_copy(
        src_ref=src, dst_ref=dst, send_sem=send_sem, recv_sem=recv_sem, device_id=(p, z), device_id_type=MESH
    )


def greet(p, z, pc, px, py):
    barrier = pltpu.get_barrier_semaphore()
    for peer in ((pc, z), (px, z), (py, z), (p, (z + 1) % 4), (p, (z + 2) % 4), (p, (z + 3) % 4)):
        pl.semaphore_signal(barrier, inc=1, device_id=peer, device_id_type=MESH)
    pl.semaphore_wait(barrier, 6)


class Gather:
    steps = [(m, d) for m in range(3) for d in (1, 3, 2)]
    sems = [(3,)] + [(3, 3)] * 12 + [(3,)] * 2

    def __init__(self, mats, whole, bias, biases, sems):
        self.mats, self.whole, self.bias, self.biases = mats, whole, bias, biases
        (self.ls, self.zs, self.zr, self.xs, self.xr, self.ys, self.yr, self.as_, self.ar, self.bs, self.br, self.cs,
         self.cr, self.ss, self.sr) = sems
        self.where = place()

    def local(self, m):
        z = self.where[1]
        return pltpu.make_async_copy(self.mats[m], self.whole.at[m, z], self.ls.at[m])

    def small(self, d):
        p, z = self.where[:2]
        return remote(self.bias, self.biases.at[z], self.ss.at[d - 1], self.sr.at[d - 1], p, (z + d) % 4)

    def along_z(self, m, d):
        p, z, core, xy = self.where[:4]
        return remote(self.mats[m].at[xy, core], self.whole.at[m, z, xy, core], self.zs.at[m, d - 1],
                      self.zr.at[m, d - 1], p, (z + d) % 4)

    def plane(self, m, d, block, rows, send_sem, recv_sem, peer):
        z = self.where[1]
        part = self.whole.at[m, (z + 4 - d) % 4, block, self.where[2], rows]
        return remote(part, part, send_sem.at[m, d - 1], recv_sem.at[m, d - 1], peer, z)

    def to_x(self, m, d):
        return self.plane(m, d, self.where[3], slice(None), self.xs, self.xr, self.where[5])

    def to_y(self, m, d):
        return self.plane(m, d, self.where[3], slice(None), self.ys, self.yr, self.where[6])

    def on_to_y(self, m, d):
        return self.plane(m, d, self.where[7], pl.ds(0, HALF), self.as_, self.ar, self.where[6])

    def on_to_x(self, m, d):
        return self.plane(m, d, self.where[8], pl.ds(HALF, HALF), self.bs, self.br, self.where[5])

    def to_core(self, m, d):
        z = self.where[1]
        part = self.whole.at[m, (z + 4 - d) % 4, :, self.where[2]]
        return remote(part, part, self.cs.at[m, d - 1], self.cr.at[m, d - 1], self.where[4], z)

    def begin(self):
        p, z, _, _, pc, px, py = self.where[:7]
        greet(p, z, pc, px, py)
        for d in (1, 3, 2):
            self.small(d).start()
            self.along_z(0, d).start()
        for m in range(3):
            self.local(m).start()
        own = pltpu.make_async_copy(self.bias, self.biases.at[z], self.ls.at[0])
        self.local(0).wait()
        own.start()
        own.wait()
        for d in (1, 2, 3):
            self.small(d).wait_recv()

    def stage(self, i):
        steps, n = self.steps, len(self.steps)
        if i < n:
            m, d = steps[i]
            self.along_z(m, d).wait_recv()
            self.to_x(m, d).start()
            self.to_y(m, d).start()
            if m < 2:
                self.along_z(m + 1, d).start()
        if 0 <= i - 1 < n:
            self.to_x(*steps[i - 1]).wait_recv()
            self.to_y(*steps[i - 1]).wait_recv()
            self.on_to_y(*steps[i - 1]).start()
            self.on_to_x(*steps[i - 1]).start()
        if 0 <= i - 2 < n:
            self.on_to_y(*steps[i - 2]).wait_recv()
            self.on_to_x(*steps[i - 2]).wait_recv()
            self.to_core(*steps[i - 2]).start()
        if 0 <= i - 3 < n:
            self.to_core(*steps[i - 3]).wait_recv()

    def finish(self):
        for m in (1, 2):
            self.local(m).wait()
        for d in (1, 2, 3):
            self.small(d).wait_send()
        for m, d in self.steps:
            for copy in (self.along_z, self.to_x, self.to_y, self.on_to_y, self.on_to_x, self.to_core):
                copy(m, d).wait_send()


def gather_kernel(p_ref, e_ref, s_ref, bias_ref, whole_ref, biases_ref, *sems):
    gather = Gather((p_ref, e_ref, s_ref), whole_ref, bias_ref, biases_ref, sems)
    gather.begin()
    for i in range(len(Gather.steps) + 3):
        gather.stage(i)
    gather.finish()


def gather_weights(mats, bias):
    if lax.axis_size("dp") != 8 or lax.axis_size("mp") != 4:
        whole = jnp.stack([lax.all_gather(m, "mp", axis=0) for m in mats])
        return whole, lax.all_gather(bias, "mp", axis=0)
    hbm = pl.BlockSpec(memory_space=pl.ANY)
    whole, biases = pl.pallas_call(
        gather_kernel,
        out_shape=(jax.ShapeDtypeStruct((3, 4, 4, 2, SLICE, D), BF), jax.ShapeDtypeStruct((4, SMALL, D), BF)),
        in_specs=[hbm] * 4,
        out_specs=(hbm, hbm),
        scratch_shapes=[pltpu.SemaphoreType.DMA(s) for s in Gather.sems],
        compiler_params=pltpu.CompilerParams(collective_id=0, has_side_effects=True),
        name="gather_weights",
    )(*[m.reshape(4, 2, SLICE, D) for m in mats], bias)
    return whole.reshape(3, 4, D, D), biases


class Scatter:
    steps = [(m, k) for m in range(3) for k in range(4)]
    buffers = [((12, 4, SLICE, D), BF)] + [((12, 2, HALF, D), BF)] * 2 + [((12, HALF, D), BF)] * 2 + [
        ((3, 3, SLICE, D), BF), ((3, 4, SLICE, D), BF), ((6, SMALL, D), F32), ((3, SMALL, D), F32)]
    sems = [(12,)] * 2 + [(12, 2)] * 4 + [(12,)] * 4 + [(3, 3)] * 2 + [(6,)] * 2

    def __init__(self, grads, buffers, sems):
        self.grads = grads
        self.sum, self.rx, self.ry, self.ra, self.rb, self.rz, self.plane, self.rv, self.sv = buffers
        (self.cs, self.cr, self.xs, self.xr, self.ys, self.yr, self.as_, self.ar, self.bs, self.br, self.zs, self.zr,
         self.ss, self.sr) = sems
        self.where = place()

    def to_core(self, i):
        m, k = self.steps[i]
        _, z, core, _, pc = self.where[:5]
        return remote(self.grads.at[m, k, :, 1 - core], self.sum.at[i], self.cs.at[i], self.cr.at[i], pc, z)

    def to_x(self, i, t):
        q = (self.where[7], 3 - self.where[3])[t]
        return remote(self.sum.at[i, q, pl.ds(0, HALF)], self.rx.at[i, t], self.xs.at[i, t], self.xr.at[i, t],
                      self.where[5], self.where[1])

    def to_y(self, i, t):
        q = (self.where[8], 3 - self.where[3])[t]
        return remote(self.sum.at[i, q, pl.ds(HALF, HALF)], self.ry.at[i, t], self.ys.at[i, t], self.yr.at[i, t],
                      self.where[6], self.where[1])

    def on_to_y(self, i):
        return remote(self.sum.at[i, self.where[8], pl.ds(0, HALF)], self.ra.at[i], self.as_.at[i], self.ar.at[i],
                      self.where[6], self.where[1])

    def on_to_x(self, i):
        return remote(self.sum.at[i, self.where[7], pl.ds(HALF, HALF)], self.rb.at[i], self.bs.at[i], self.br.at[i],
                      self.where[5], self.where[1])

    def along_z(self, m, d):
        p, z = self.where[:2]
        k = (z + d) % 4
        return remote(self.plane.at[m, k], self.rz.at[m, d - 1], self.zs.at[m, d - 1], self.zr.at[m, d - 1], p, k)

    def begin(self):
        p, z, _, _, pc, px, py = self.where[:7]
        greet(p, z, pc, px, py)

    def stage(self, i):
        n = len(self.steps)
        core, xy, xyx, xyy = self.where[2], self.where[3], self.where[7], self.where[8]
        low, high = slice(0, HALF), slice(HALF, SLICE)
        if i < n:
            self.to_core(i).start()
        j = i - 1
        if 0 <= j < n:
            self.to_core(j).wait_recv()
            m, k = self.steps[j]
            for q in range(4):
                self.sum[j, q] = (self.sum[j, q].astype(F32) + self.grads[m, k, q, core].astype(F32)).astype(BF)
            for t in (0, 1):
                self.to_x(j, t).start()
                self.to_y(j, t).start()
        j = i - 2
        if 0 <= j < n:
            for t in (0, 1):
                self.to_x(j, t).wait_recv()
                self.to_y(j, t).wait_recv()
            self.sum[j, xyy, low] = (self.sum[j, xyy, low].astype(F32) + self.rx[j, 1].astype(F32)).astype(BF)
            self.sum[j, xyx, high] = (self.sum[j, xyx, high].astype(F32) + self.ry[j, 1].astype(F32)).astype(BF)
            self.on_to_y(j).start()
            self.on_to_x(j).start()
        j = i - 3
        if 0 <= j < n:
            m, k = self.steps[j]
            self.on_to_y(j).wait_recv()
            self.on_to_x(j).wait_recv()
            self.plane[m, k, low] = (
                self.sum[j, xy, low].astype(F32) + self.rx[j, 0].astype(F32) + self.ra[j].astype(F32)
            ).astype(BF)
            self.plane[m, k, high] = (
                self.sum[j, xy, high].astype(F32) + self.ry[j, 0].astype(F32) + self.rb[j].astype(F32)
            ).astype(BF)
            if k == 3:
                for d in (1, 2, 3):
                    self.along_z(m, d).start()

    def total(self, m):
        for d in (1, 2, 3):
            self.along_z(m, d).wait_recv()
        own = self.plane[m, self.where[1]].astype(F32)
        return own + self.rz[m, 0].astype(F32) + self.rz[m, 1].astype(F32) + self.rz[m, 2].astype(F32)

    def small_to(self, s, src, p, z):
        return remote(src, self.rv.at[s], self.ss.at[s], self.sr.at[s], p, z)

    def small_copy(self, part, c):
        p, z, _, _, pc, px, py = self.where[:7]
        if c == 0:
            return self.small_to(0, part, pc, z)
        if c == 1:
            return self.small_to(1, self.sv.at[0], px, z)
        if c == 2:
            return self.small_to(2, self.sv.at[1], py, z)
        return self.small_to(c, self.sv.at[2], p, (z + c - 2) % 4)

    def small_stage(self, part, i):
        if i == 0:
            self.small_copy(part, 0).start()
        elif i < 4:
            self.small_copy(part, i - 1).wait_recv()
            before = part[...] if i == 1 else self.sv[i - 2]
            self.sv[i - 1] = before + self.rv[i - 1]
            for c in (i,) if i < 3 else (3, 4, 5):
                self.small_copy(part, c).start()
        else:
            for c in (3, 4, 5):
                self.small_copy(part, c).wait_recv()
            return self.sv[2] + self.rv[3] + self.rv[4] + self.rv[5]

    def finish(self, part):
        for c in range(6):
            self.small_copy(part, c).wait_send()
        for i in range(len(self.steps)):
            self.to_core(i).wait_send()
            self.on_to_y(i).wait_send()
            self.on_to_x(i).wait_send()
            for t in (0, 1):
                self.to_x(i, t).wait_send()
                self.to_y(i, t).wait_send()
        for m in range(3):
            for d in (1, 2, 3):
                self.along_z(m, d).wait_send()


def scatter_kernel(grads_ref, part_ref, out_ref, small_ref, held, load_sem, *rest):
    buffers, sems = rest[: len(Scatter.buffers)], rest[len(Scatter.buffers) :]
    scatter = Scatter(held, buffers, sems)
    n = len(Scatter.steps)

    def load(i):
        m, k = Scatter.steps[i]
        return pltpu.make_async_copy(grads_ref.at[m, k], held.at[m, k], load_sem.at[i])

    scatter.begin()
    for i in range(n):
        load(i).start()
    for i in range(n + 3):
        if i < n:
            load(i).wait()
        scatter.stage(i)
        if i in (0, 2, 4, 6, 8):
            total = scatter.small_stage(part_ref, i // 2)
            if i == 8:
                small_ref[...] = total
    for m in range(3):
        out_ref[m] = scatter.total(m)
    scatter.finish(part_ref)


def scatter_gradients(grads, part):
    if lax.axis_size("dp") != 8 or lax.axis_size("mp") != 4:
        grads = lax.psum_scatter(grads, "dp", scatter_dimension=2, tiled=True)
        grads = lax.psum_scatter(grads, "mp", scatter_dimension=1, tiled=True)
        return grads[:, 0].astype(F32), lax.psum(part, ("dp", "mp"))
    hbm, vmem = pl.BlockSpec(memory_space=pl.ANY), pl.BlockSpec(memory_space=pltpu.VMEM)
    return pl.pallas_call(
        scatter_kernel,
        out_shape=(jax.ShapeDtypeStruct((3, SLICE, D), F32), jax.ShapeDtypeStruct((SMALL, D), F32)),
        in_specs=[hbm, vmem],
        out_specs=(vmem, vmem),
        scratch_shapes=[pltpu.VMEM((3, 4, 4, 2, SLICE, D), BF), pltpu.SemaphoreType.DMA((12,))]
        + [pltpu.VMEM(s, t) for s, t in Scatter.buffers]
        + [pltpu.SemaphoreType.DMA(s) for s in Scatter.sems],
        compiler_params=pltpu.CompilerParams(collective_id=1, has_side_effects=True, vmem_limit_bytes=56 << 20),
        name="scatter_gradients",
    )(grads.reshape(3, 4, 4, 2, SLICE, D), part)


def mm(a, b, dims):
    return lax.dot_general(a, b, (dims, ((), ())), preferred_element_type=jnp.float32)


def pack_weights(triple_weight, output_weight, expand_weight, shrink_weight):
    width = triple_weight.shape[2]
    mixing = jnp.concatenate([triple_weight.transpose(1, 0, 2).reshape(D, 3 * width), output_weight.T], axis=1)
    return mixing, expand_weight, shrink_weight


def pack_biases(query_value_bias, expand_bias):
    pair = query_value_bias.reshape(2, -1)
    width = pair.shape[1]
    none = jnp.zeros((width,), BF)
    first = jnp.concatenate([pair[0], none, pair[1], none])
    return jnp.concatenate([first[None], expand_bias.reshape(1, -1), jnp.zeros((SMALL - 2, D), BF)])


def update_all(state, reduced, sums, activations_shape, outs):
    dp, mp = lax.axis_index("dp"), lax.axis_index("mp")
    groups, parts = lax.axis_size("mp"), lax.axis_size("dp")
    heads = D // HEAD
    width = D // (groups * parts)
    vec = lax.dynamic_slice_in_dim(sums[:6], (dp * groups + mp) * width, width, 1)
    qv = sums[6:8].reshape(2, heads, HEAD)
    qv = lax.dynamic_slice_in_dim(qv, mp * (heads // groups), heads // groups, 1)
    qv = lax.dynamic_slice_in_dim(qv, dp * (HEAD // parts), HEAD // parts, 2)
    eb = sums[8:12].reshape(FF // HEAD, HEAD)
    eb = lax.dynamic_slice_in_dim(eb, mp * (FF // HEAD // groups), FF // HEAD // groups, 0)
    eb = lax.dynamic_slice_in_dim(eb, dp * (HEAD // parts), HEAD // parts, 1)
    cut = 3 * D // groups
    rows = reduced.shape[1]
    triple_grad = reduced[0, :, :cut].reshape(rows, 3, D // groups).transpose(1, 0, 2)
    grads = (triple_grad, qv, reduced[0, :, cut:].T, reduced[1], eb, reduced[2].T, vec)
    rates = (D ** (-0.5), 0.5, (D // 16) ** (-0.5), D ** (-0.5), 0.5, FF ** (-0.5), 0.3)
    for i in range(7):
        outs = outs + adam_update(state[3 * i], state[3 * i + 1], state[3 * i + 2], grads[i], rates[i])
    return outs


def per_device(
    activations,
    cotangent,
    segments,
    triple_weight,
    query_value_bias,
    output_weight,
    expand_weight,
    expand_bias,
    shrink_weight,
    vector_params,
    *state,
):
    rows, length, _ = activations.shape
    tokens = rows * length
    groups = lax.axis_size("mp")
    heads = D // HEAD
    width = D // groups
    mats = pack_weights(triple_weight, output_weight, expand_weight, shrink_weight)
    whole, biases = gather_weights(mats, pack_biases(query_value_bias, expand_bias))
    biases = biases.astype(F32)
    gains = vector_params.astype(jnp.float32)
    seg = lax.dynamic_slice_in_dim(segments, lax.axis_index("mp") * rows, rows, 0)
    allowed = (seg[:, :, None] == seg[:, None, :])[:, None]
    x = activations.reshape(tokens, D)
    back = cotangent.reshape(tokens, D).astype(jnp.float32)
    mixing, expand, shrink = whole[0], whole[1], whole[2]
    triple = mixing[:, :, : 3 * width]
    output = mixing[:, :, 3 * width :]

    proj = jnp.einsum("td,zde->zte", x, triple, preferred_element_type=F32)
    proj = (proj + biases[:, None, 0, : 3 * width]).astype(BF)
    proj = proj.reshape(groups, rows, length, 3, heads // groups, HEAD)
    q4, k4, v4 = (proj[:, :, :, j] for j in range(3))
    scores = jnp.einsum("zrqhc,zrkhc->rzhqk", q4, k4, preferred_element_type=F32) * HEAD ** (-0.5)
    scores = jnp.where(allowed[:, None], scores, MASKED)
    row_max = jnp.max(scores, axis=-1, keepdims=True)
    weights = jnp.exp(scores - row_max)
    probs = weights / jnp.sum(weights, axis=-1, keepdims=True)
    probs_low = probs.astype(BF)
    context = jnp.einsum("rzhqk,zrkhc->zrqhc", probs_low, v4, preferred_element_type=F32)
    context = context.astype(BF).reshape(groups, tokens, width)
    attended = jnp.einsum("zte,zde->td", context, output, preferred_element_type=F32)
    mixed = x.astype(F32) + attended + gains[2]
    hidden, normed_one, scale_one = norm_forward(mixed, gains[0], gains[1])
    hidden_low = hidden.astype(BF)
    expanded = jnp.einsum("td,zdf->ztf", hidden_low, expand, preferred_element_type=F32) + biases[:, None, 1]
    cumulative = 0.5 * (1.0 + jax.scipy.special.erf(expanded * SQRT_HALF))
    active = (expanded * cumulative).astype(BF)
    slope = (cumulative + expanded * jnp.exp(-0.5 * expanded * expanded) * INV_ROOT_TAU).astype(BF)
    shrunk = jnp.einsum("ztf,zfd->td", active, shrink, preferred_element_type=F32)
    summed = hidden + shrunk + gains[5]
    result, normed_two, scale_two = norm_forward(summed, gains[3], gains[4])
    dsummed = norm_backward(back, gains[3], normed_two, scale_two)
    dsummed_low = dsummed.astype(BF)

    shrink_grad = jnp.einsum("td,ztf->zdf", dsummed_low, active, preferred_element_type=F32).astype(BF)
    dactive = jnp.einsum("td,zfd->ztf", dsummed_low, shrink, preferred_element_type=F32)
    dexpanded = (dactive * slope).astype(BF)
    expand_grad = jnp.einsum("td,ztf->zdf", hidden_low, dexpanded, preferred_element_type=F32).astype(BF)
    dhidden = dsummed + jnp.einsum("ztf,zdf->td", dexpanded, expand, preferred_element_type=F32)
    dmixed = norm_backward(dhidden, gains[0], normed_one, scale_one)
    dmixed_low = dmixed.astype(BF)
    output_grad = jnp.einsum("td,zte->zde", dmixed_low, context, preferred_element_type=F32).astype(BF)
    dcontext = jnp.einsum("td,zde->zte", dmixed_low, output, preferred_element_type=F32).astype(BF)
    dcontext = dcontext.reshape(groups, rows, length, heads // groups, HEAD)
    dvalue = jnp.einsum("rzhqk,zrqhc->zrkhc", probs_low, dcontext, preferred_element_type=F32)
    dprobs = jnp.einsum("zrqhc,zrkhc->rzhqk", dcontext, v4, preferred_element_type=F32)
    inner = jnp.sum(probs * dprobs, axis=-1, keepdims=True)
    dscores = (probs * (dprobs - inner)).astype(BF)
    dquery = jnp.einsum("rzhqk,zrkhc->zrqhc", dscores, k4, preferred_element_type=F32) * HEAD ** (-0.5)
    dkey = jnp.einsum("rzhqk,zrqhc->zrkhc", dscores, q4, preferred_element_type=F32) * HEAD ** (-0.5)
    dproj = jnp.stack([dquery, dkey, dvalue], axis=3).astype(BF).reshape(groups, tokens, 3 * width)
    triple_grad = jnp.einsum("td,zte->zde", x, dproj, preferred_element_type=F32).astype(BF)
    input_grad = dmixed + jnp.einsum("zte,zde->td", dproj, triple, preferred_element_type=F32)

    def total(t):
        return jnp.sum(t.astype(F32), axis=0)

    dsum = jnp.sum(dproj.astype(F32), axis=1)
    part = jnp.stack([
        total(dhidden * normed_one), total(dhidden), total(dmixed),
        total(back * normed_two), total(back), total(dsummed),
        dsum[:, :width].reshape(-1), dsum[:, 2 * width :].reshape(-1),
    ])
    part = jnp.concatenate([part, jnp.sum(dexpanded.astype(F32), axis=1), jnp.zeros((SMALL - 12, D), F32)])
    grads = jnp.stack([jnp.concatenate([triple_grad, output_grad], axis=2), expand_grad, shrink_grad])
    reduced, sums = scatter_gradients(grads, part)
    outs = (result.astype(BF).reshape(activations.shape), input_grad.reshape(activations.shape))
    return update_all(state, reduced, sums, activations.shape, outs)


STATE_SPECS = (
    P(None, "dp", "mp"),
    P(None, "mp", "dp"),
    P("mp", "dp"),
    P("dp", "mp"),
    P("mp", "dp"),
    P("mp", "dp"),
    P(None, ("dp", "mp")),
)


def solution(mesh):
    rows = P(("dp", "mp"), None, None)
    placed = (
        rows,
        rows,
        P("dp", None),
        P(None, None, "mp"),
        P(None, "mp", None),
        P("mp", None),
        P(None, "mp"),
        P("mp", None),
        P("mp", None),
        P(),
    )
    for spec in STATE_SPECS:
        placed = placed + (spec,) * 3
    out_specs = (rows, rows)
    for spec in STATE_SPECS:
        out_specs = out_specs + (spec,) * 4
    return jax.shard_map(per_device, mesh=mesh, in_specs=placed, out_specs=out_specs, check_vma=False)
```

time: 657 us -> 623 us (0.948)
  Pallas kernels: 0 us -> 249 us
  waiting for transfers between devices: 142 us -> 0 us
  blocking collectives: 133 us -> 0 us
  other arithmetic: 61.6 us -> 105 us
  matrix products: 189 us -> 155 us
  between operations: 15.1 us -> 2.02 us
    pallas_call x0 -> x2, Pallas kernels: none -> 249 us  [the longest x1 164 us: gather_weights(): pl.pallas_call(gather_kernel, out_shape=(jax.ShapeDtypeStruct((3, 4, 4, 2...]
    reduce_scatter x6 -> x0, waiting for transfers between devices: 104 us -> none  [the longest x3 56.5 us: reduce_grad(): lax.psum_scatter(part, 'mp', scatter_dimension=part.ndim - 1, tiled=True)]
    all_gather x6 -> x0, blocking collectives: 93.6 us -> none  [the longest x1 21.7 us: per_device(): lax.all_gather(triple, 'mp', axis=2, tiled=True)]
    psum x1 -> x0, blocking collectives: 39.7 us -> none  [per_device(): lax.psum(jnp.concatenate([vector_grad, total(dexpanded).reshape(4, D)]),...]
    unnamed x14 -> x0, waiting for transfers between devices: 37.4 us -> none
    dot_general x24 -> x18, matrix products: 189 us -> 155 us  [the longest x1 16.3 us: per_device(): jnp.einsum('td,zfd->ztf', dsummed_low, shrink, preferred_element_type=F32)]
    sub x0 -> x1, other arithmetic: none -> 32.5 us  [per_device(): dscores = (probs * (dprobs - inner)).astype(BF)]
    unnamed x109 -> x159, local copies, waits for them, and re-layouts: 41.8 us -> 18.7 us
  transfers between devices with their start and end apart: 12 -> 0, of which waited for: 7 -> 0; matrix products, arithmetic and copies ran while one was open for 36% -> 0% of each run, Pallas kernels for 0% -> 0%
where the time goes in v2:
time: 623 us; the launch traced here: 614 us
  Pallas kernels  249 us (40%)
  matrix products  155 us (25%)
  other arithmetic  105 us (17%)
  local copies, waits for them, and re-layouts  103 us (17%)
    pallas_call x1, Pallas kernels, gather_weights(): pl.pallas_call(gather_kernel, out_shape=(jax.ShapeDtypeStruct((3, 4, 4, 2...  164 us
    pallas_call x1, Pallas kernels, scatter_gradients(): pl.pallas_call(scatter_kernel, out_shape=(jax.ShapeDtypeStruct((3, SLICE,...  84.9 us
    sub x1, other arithmetic, per_device(): dscores = (probs * (dprobs - inner)).astype(BF)  32.5 us
    sub x1, other arithmetic, per_device(): weights = jnp.exp(scores - row_max)  24.8 us
    convert_element_type x2, local copies, waits for them, and re-layouts, per_device(): jnp.stack([dquery, dkey, dvalue], axis=3).astype(BF)  24.5 us
    unnamed x159, local copies, waits for them, and re-layouts  18.7 us
    dot_general x1, matrix products, per_device(): jnp.einsum('td,zfd->ztf', dsummed_low, shrink, preferred_element_type=F32)  16.3 us
    reshape x1, local copies, waits for them, and re-layouts, per_device(): proj = proj.reshape(groups, rows, length, 3, heads // groups, HEAD)  13.9 us

profile of v2, /device:TPU:0, one launch (start us, length us, event | category | flops | bytes accessed | tf_op | source)
XLA Modules:
  0.0 613.9 jit_solution(2731855136989388419)
XLA Ops:
  2.0 1.1 copy.148
  3.2 4.4 concatenate.21
  7.6 1.7 copy.149
  9.3 1.2 pad_maximum_fusion.2.p_ref
  11.7 164.2 %gather_weights.1 = (bf16[3,4,4,2,96,768]{5,4,3,2,1,0:T(8,128)(2,1)}, bf16[4,16,768]{2,1,0:T(8,128)(2,1)}) custom-call(bf16[4,2,96,768]{3,2,1,0:T(8,128)(2,1)} %pad_maximum_fusion.2.p_ref, bf16[4,2,96,768]{3,2,1,0:T(8,128)(2,1)} %bitcast.234, bf16[4,2,96,768]{3,2,1,0:T(8,128)(2,1)} %bitcast.235, bf16[16,768]{1,0:T(8,128)(2,1)} %maximum_maximum_fusion.bias_ref), custom_call_target="tpu_custom_call" | custom-call | tf_op jit(solution)/shard_map/gather_weights/pallas_call | solution.py:178
  175.8 0.8 slice.125
  176.7 10.1 %fusion.119 = (bf16[1,4,4,2,96,768]{5,4,3,2,1,0:T(8,128)(2,1)}, bf16[1,4,4,2,96,768]{5,4,3,2,1,0:T(8,128)(2,1)}, bf16[1,4,4,2,96,768]{5,4,3,2,1,0:T(8,128)(2,1)S(1)}) fusion(bf16[3,4,4,2,96,768]{5,4,3,2,1,0:T(8,128)(2,1)} %get-tuple-element.34), kind=kLoop, calls=%fused_computation.184 | loop fusion | bytes 28311552 | tf_op jit(solution)/shard_map/slice | solution.py:432
  186.8 0.8 slice.118
  187.6 1.4 copy-done.12
  189.0 7.5 %fusion.27 = bf16[4,1152,576]{1,2,0:T(8,128)(2,1)} fusion(f32[4,576]{1,0:T(4,128)S(1)} %bitcast.240, bf16[1152,768,1]{1,0,2:T(8,128)(2,1)S(1)} %bitcast.242, bf16[4,768,768]{2,1,0:T(8,128)(2,1)S(1)} %bitcast.215), kind=kOutput, calls=%fused_computation.42 | convolution fusion | flops 4082171904 | bytes 11020288 | tf_op jit(solution)/shard_map/td,zde->zte/dot_general | solution.py:436
  196.5 13.9 %reshape.192 = bf16[4,4,288,3,3,64]{2,1,5,4,3,0:T(4,128)(2,1)} reshape(bf16[4,1152,576]{1,2,0:T(8,128)(2,1)} %fusion.27) | data formatting | bytes 10616832 | tf_op jit(solution)/shard_map/reshape | solution.py:438
  210.4 4.8 fusion.120
  215.3 9.2 %fusion.52 = f32[4,4,3,288,288]{3,4,2,1,0:T(8,128)} fusion(bf16[4,4,288,1,3,64]{2,1,5,4,3,0:T(4,128)(2,1)S(1)} %get-tuple-element.174, bf16[4,4,288,1,3,64]{2,1,5,4,3,0:T(4,128)(2,1)S(1)} %get-tuple-element.175), kind=kOutput, calls=%fused_computation.90 | convolution fusion | flops 509607936 | bytes 19464192 | tf_op jit(solution)/shard_map/zrqhc,zrkhc->rzhqk/dot_general | solution.py:440
  224.8 24.8 %fusion.122 = (f32[4,4,3,288]{3,2,1,0:T(4,128)S(1)}, f32[4,4,3,288,288]{3,4,2,1,0:T(8,128)}) fusion(f32[4,4,3,288,288]{3,4,2,1,0:T(8,128)} %fusion.52, pred[4,288,288]{1,2,0:T(8,128)(4,1)S(1)} %broadcast_compare_fusion), kind=kOutput, calls=%fused_computation.187 | output fusion | flops 23888160 | bytes 32237568 | tf_op jit(solution)/shard_map/sub | solution.py:443
  249.6 8.5 %fusion.102 = bf16[4,4,3,288,288]{3,4,2,1,0:T(8,128)(2,1)S(1)} fusion(f32[4,4,3,288,288]{3,4,2,1,0:T(8,128)} %get-tuple-element.188, f32[4,4,3,288]{3,2,1,0:T(4,128)S(1)} %get-tuple-element.187), kind=kLoop, calls=%fused_computation.174 | loop fusion | flops 7962624 | bytes 23943168 | tf_op jit(solution)/shard_map/convert_element_type | solution.py:445
  258.2 2.4 convert_bitcast_fusion.1
  260.6 1.4 copy-done.5
  262.0 1.8 copy.155
  263.8 2.7 reshape.193
  266.5 5.6 fusion.123
  272.8 13.9 %fusion.13 = (bf16[4,1152,768]{1,2,0:T(8,128)(2,1)}, f32[4,768,1152]{2,1,0:T(8,128)}) fusion(f32[4,768]{1,0:T(4,128)S(1)} %bitcast.238, bf16[4,768,768]{2,1,0:T(8,128)(2,1)S(1)} %bitcast.221, f32[1152,768]{1,0:T(8,128)S(1)} %get-tuple-element.190, f32[768]{0:T(1024)S(1)} %get-tuple-element.139, f32[1152]{0:T(1024)S(1)} %add_rsqrt_fusion.1, ...), kind=kOutput, calls=%fused_computation.23 | convolution fusion | flops 5461475328 | bytes 29518848 | tf_op jit(solution)/shard_map/td,zdf->ztf/dot_general | solution.py:452
  286.7 8.7 %fusion.124 = (f32[1152]{0:T(1024)S(1)}, f32[1152,768]{1,0:T(8,128)S(1)}) fusion(f32[768]{0:T(1024)S(1)} %copy-done.57, bf16[4,1152,768]{1,2,0:T(8,128)(2,1)} %get-tuple-element.191, bf16[4,768,768]{2,1,0:T(8,128)(2,1)S(1)} %bitcast.228, f32[768]{0:T(1024)} %copy-done.55, f32[1152]{0:T(1024)S(1)} %add_rsqrt_fusion.1, ...), kind=kOutput, calls=%fused_computation.189 | convolution fusion | flops 5442010112 | bytes 18897408 | tf_op jit(solution)/shard_map/ztf,zfd->td/dot_general | solution.py:456
  296.0 0.9 copy-done.2
  296.9 1.8 fusion.40
  299.4 1.6 convert_reduce_fusion.2
  301.5 1.4 div.146
  302.9 4.5 fusion.116
  307.4 16.3 %convert_reduce_fusion = (f32[4,768]{1,0:T(4,128)}, bf16[4,1152,768]{1,2,0:T(8,128)(2,1)}) fusion(f32[4,768,1152]{2,1,0:T(8,128)} %get-tuple-element.192, f32[4,768]{1,0:T(4,128)S(1)} %bitcast.239, bf16[4,768,768]{2,1,0:T(8,128)(2,1)} %bitcast.225, f32[1152,768]{1,0:T(8,128)S(1)} %get-tuple-element.167), kind=kOutput, calls=%fused_computation.24 | convolution fusion | flops 5489783808 | bytes 29515776 | tf_op jit(solution)/shard_map/td,zfd->ztf/dot_general | solution.py:463
  323.7 10.0 %multiply_reduce_fusion.1 = (f32[768]{0:T(1024)}, f32[1152]{0:T(1024)S(1)}, f32[1152]{0:T(1024)S(1)}, f32[768]{0:T(1024)}, f32[1152,768]{1,0:T(8,128)S(1)}) fusion(f32[1152,768]{1,0:T(8,128)S(1)} %copy-done.4, f32[1152]{0:T(1024)S(1)} %copy-done.34, f32[1152]{0:T(1024)S(1)} %broadcast_multiply_fusion.8, f32[768]{0:T(1024)S(1)} %copy-done.39, ...), kind=kOutput, calls=%fused_computation.64 | convolution fusion | flops 5444661248 | bytes 22440960 | tf_op jit(solution)/shard_map/ztf,zdf->td/dot_general | solution.py:466
  333.8 1.8 fusion.118
  335.6 1.8 copy-done.14
  337.4 5.4 fusion.44
  342.8 6.0 reshape.195
  348.8 10.0 %fusion.55 = bf16[4,4,288,1,3,64]{2,5,4,1,0,3:T(8,128)(2,1)} fusion(bf16[4,4,3,288,288]{3,4,2,1,0:T(8,128)(2,1)} %copy-done.5, bf16[4,4,288,3,64]{2,1,4,3,0:T(4,128)(2,1)} %reshape.195), kind=kOutput, calls=%fused_computation.96 | convolution fusion | flops 509607936 | bytes 11501568 | tf_op jit(solution)/shard_map/rzhqk,zrqhc->zrkhc/dot_general | solution.py:472
  358.8 8.7 %fusion.47 = f32[4,4,3,288,288]{3,4,2,1,0:T(8,128)} fusion(bf16[4,4,288,1,3,64]{2,1,5,4,3,0:T(4,128)(2,1)S(1)} %copy-done.10, bf16[4,4,288,3,64]{2,1,4,3,0:T(4,128)(2,1)S(1)} %copy-done.11), kind=kOutput, calls=%fused_computation.84 | convolution fusion | flops 509607936 | bytes 19464192 | tf_op jit(solution)/shard_map/zrqhc,zrkhc->rzhqk/dot_general | solution.py:473
  367.4 32.5 %multiply_convert_fusion = bf16[4,4,3,288,288]{3,4,2,1,0:T(8,128)(2,1)} fusion(f32[4,4,3,288,288]{3,4,2,1,0:T(8,128)} %fusion.47, f32[4,4,3,288,288]{3,4,2,1,0:T(8,128)} %get-tuple-element.188, f32[4,4,3,288]{3,2,1,0:T(4,128)} %copy-done.27), kind=kOutput, calls=%fused_computation.2 | output fusion | flops 23901984 | bytes 39868416 | tf_op jit(solution)/shard_map/sub | solution.py:475
  399.9 10.0 %multiply_bitcast_fusion = bf16[4,4,288,1,3,64]{2,5,4,1,0,3:T(8,128)(2,1)} fusion(bf16[4,4,3,288,288]{3,4,2,1,0:T(8,128)(2,1)} %multiply_convert_fusion, bf16[4,4,288,1,3,64]{2,1,5,4,3,0:T(4,128)(2,1)} %copy-done.8), kind=kOutput, calls=%fused_computation.40 | convolution fusion | flops 511377408 | bytes 11501568 | tf_op jit(solution)/shard_map/rzhqk,zrqhc->zrkhc/dot_general | solution.py:477
  409.9 6.4 %multiply_bitcast_fusion.1 = bf16[4,4,288,1,3,64]{2,5,4,1,0,3:T(8,128)(2,1)S(1)} fusion(bf16[4,4,3,288,288]{3,4,2,1,0:T(8,128)(2,1)} %multiply_convert_fusion, bf16[4,4,288,1,3,64]{2,1,5,4,3,0:T(4,128)(2,1)S(1)} %copy-done.7), kind=kOutput, calls=%fused_computation.41 | convolution fusion | flops 511377408 | bytes 11501568 | tf_op jit(solution)/shard_map/rzhqk,zrkhc->zrqhc/dot_general | solution.py:476
  416.4 4.7 convert_reduce_fusion.1
  421.1 12.6 %copy.168 = bf16[4,4,288,3,3,64]{2,1,5,4,3,0:T(4,128)(2,1)} copy(bf16[4,4,288,3,3,64]{2,5,4,1,0,3:T(8,128)(2,1)} %get-tuple-element.165) | data formatting | bytes 10616832 | tf_op jit(solution)/shard_map/convert_element_type | solution.py:478
  433.6 11.9 %convert_element_type.157 = bf16[4,1152,576]{1,2,0:T(8,128)(2,1)} reshape(bf16[4,4,288,3,3,64]{2,1,5,4,3,0:T(4,128)(2,1)} %copy.168) | data formatting | bytes 10616832 | tf_op jit(solution)/shard_map/convert_element_type | solution.py:478
  445.6 11.4 %fusion.28 = f32[1152,768]{1,0:T(8,128)} fusion(f32[1152,768]{1,0:T(8,128)} %copy-done.14, bf16[4,1152,576]{1,2,0:T(8,128)(2,1)} %convert_element_type.157, bf16[4,768,768]{2,1,0:T(8,128)(2,1)} %bitcast.218), kind=kOutput, calls=%fused_computation.44 | convolution fusion | flops 4077748224 | bytes 16318464 | tf_op jit(solution)/shard_map/zte,zde->td/dot_general | solution.py:480
  456.9 1.8 copy.179
  458.7 11.2 %convolution_convert_fusion.1 = bf16[4,768,768]{1,2,0:T(8,128)(2,1)} fusion(bf16[4,1152,768]{1,2,0:T(8,128)(2,1)} %get-tuple-element.191, f32[1152,768]{1,0:T(8,128)} %copy-done.13), kind=kOutput, calls=%fused_computation.80 | convolution fusion | flops 5439062016 | bytes 15335424 | tf_op jit(solution)/shard_map/td,ztf->zdf/dot_general | solution.py:462
  469.9 11.4 %convolution_convert_fusion.2 = bf16[4,768,768]{1,2,0:T(8,128)(2,1)} fusion(bf16[4,1152,768]{1,2,0:T(8,128)(2,1)} %get-tuple-element.197, f32[1152,768]{1,0:T(8,128)S(1)} %copy-done.4, f32[768]{0:T(1024)S(1)} %copy-done.56, f32[1152]{0:T(1024)S(1)} %copy-done.34, f32[1152]{0:T(1024)S(1)} %broadcast_multiply_fusion.8, f32[768]{0:T(1024)S(1)} %copy-done.40), kind=kOutput, calls=%fused_computation.81 | convolution fusion | flops 5442600960 | bytes 15350784 | tf_op jit(solution)/shard_map/td,ztf->zdf/dot_general | solution.py:465
  481.4 1.7 fusion.79
  483.1 5.2 convert_bitcast_fusion
  488.3 2.4 pad_maximum_fusion.1
  490.8 6.6 %copy.169 = bf16[4,768,768]{2,1,0:T(8,128)(2,1)} copy(bf16[4,768,768]{1,2,0:T(8,128)(2,1)} %pad_maximum_fusion.1) | data formatting | bytes 9437184 | tf_op jit(solution)/shard_map/concatenate | solution.py:492
  497.5 10.6 %pad_maximum_fusion.grads_ref = bf16[3,4,4,2,96,768]{5,4,3,2,1,0:T(8,128)(2,1)} fusion(bf16[1,4,4,2,96,768]{5,4,3,2,1,0:T(8,128)(2,1)} %bitcast.229, bf16[1,4,4,2,96,768]{5,4,3,2,1,0:T(8,128)(2,1)} %bitcast.230, bf16[1,4,4,2,96,768]{5,4,3,2,1,0:T(8,128)(2,1)} %bitcast.212), kind=kLoop, calls=%fused_computation.15 | loop fusion | flops 14155776 | bytes 28311552 | tf_op jit(solution)/shard_map/stack | solution.py:492
  508.5 1.3 concatenate.27.part_ref
  509.8 84.9 %scatter_gradients.1 = (f32[3,96,768]{2,1,0:T(8,128)}, f32[16,768]{1,0:T(8,128)}) custom-call(bf16[3,4,4,2,96,768]{5,4,3,2,1,0:T(8,128)(2,1)} %pad_maximum_fusion.grads_ref, f32[16,768]{1,0:T(8,128)} %concatenate.27.part_ref), custom_call_target="tpu_custom_call" | custom-call | tf_op jit(solution)/shard_map/scatter_gradients/pallas_call | solution.py:353
  594.8 1.0 slice.108
  596.6 0.9 copy.189
  597.5 0.9 copy.190
  598.4 0.9 copy.191
  599.3 0.8 copy.192
  600.2 0.8 fusion.113
  603.4 1.0 copy.184
  604.3 1.0 copy.185
  605.5 0.7 copy.197
  606.2 0.7 copy.198
  608.5 2.2 fusion.109
  611.6 1.2 fusion.105
  (196 shorter events, 12.1 us)
Async XLA Ops:
  0.7 223.8 %copy-start = (s32[16,288]{1,0:T(8,128)S(1)}, s32[16,288]{1,0:T(8,128)}, u32[]{:S(2)}) copy-start(s32[16,288]{1,0:T(8,128)} %param.33) | copy-start | bytes 55300
  2.0 270.7 %copy-start.38 = (f32[768]{0:T(1024)}, f32[768]{0:T(1024)S(1)}, u32[]{:S(2)}) copy-start(f32[768]{0:T(1024)S(1)} %get-tuple-element.141) | copy-start | bytes 9220
  2.0 270.7 %copy-start.55 = (f32[768]{0:T(1024)}, f32[768]{0:T(1024)S(1)}, u32[]{:S(2)}) copy-start(f32[768]{0:T(1024)S(1)} %get-tuple-element.139) | copy-start | bytes 9220
  3.2 7.3 %copy-start.52 = (bf16[12,64]{1,0:T(8,128)(2,1)S(1)}, bf16[12,64]{1,0:T(8,128)(2,1)}, u32[]{:S(2)}) copy-start(bf16[12,64]{1,0:T(8,128)(2,1)} %param.38) | copy-start | bytes 4612
  3.2 7.4 %copy-start.45 = (bf16[2,3,64]{2,0,1:T(2,128)(2,1)S(1)}, bf16[2,3,64]{2,0,1:T(2,128)(2,1)}, u32[]{:S(2)}) copy-start(bf16[2,3,64]{2,0,1:T(2,128)(2,1)} %param.35) | copy-start | bytes 2308
  176.7 96.1 %copy-start.43 = (f32[4,1,768]{2,0,1:T(4,128)}, f32[4,1,768]{2,0,1:T(4,128)S(1)}, u32[]{:S(2)}) copy-start(f32[4,1,768]{2,0,1:T(4,128)S(1)} %copy.296) | copy-start | bytes 36868
  176.7 12.3 %copy-start.59 = (bf16[4,288,768]{2,1,0:T(8,128)(2,1)S(1)}, bf16[4,288,768]{2,1,0:T(8,128)(2,1)}, u32[]{:S(2)}) copy-start(bf16[4,288,768]{2,1,0:T(8,128)(2,1)} %param.31) | copy-start | bytes 5308420
  215.3 9.2 %copy-start.6 = (bf16[4,4,288,1,3,64]{2,1,5,4,3,0:T(4,128)(2,1)}, bf16[4,4,288,1,3,64]{2,1,5,4,3,0:T(4,128)(2,1)S(1)}, u32[]{:S(2)}) copy-start(bf16[4,4,288,1,3,64]{2,1,5,4,3,0:T(4,128)(2,1)S(1)} %get-tuple-element.174) | copy-start | bytes 5308420
  215.3 9.2 %copy-start.8 = (bf16[4,4,288,1,3,64]{2,1,5,4,3,0:T(4,128)(2,1)}, bf16[4,4,288,1,3,64]{2,1,5,4,3,0:T(4,128)(2,1)S(1)}, u32[]{:S(2)}) copy-start(bf16[4,4,288,1,3,64]{2,1,5,4,3,0:T(4,128)(2,1)S(1)} %get-tuple-element.175) | copy-start | bytes 5308420
  215.3 42.9 %copy-start.9 = (bf16[4,4,288,1,3,64]{2,1,5,4,3,0:T(4,128)(2,1)}, bf16[4,4,288,1,3,64]{2,1,5,4,3,0:T(4,128)(2,1)S(1)}, u32[]{:S(2)}) copy-start(bf16[4,4,288,1,3,64]{2,1,5,4,3,0:T(4,128)(2,1)S(1)} %get-tuple-element.173) | copy-start | bytes 5308420
  249.6 8.5 %copy-start.27 = (f32[4,4,3,288]{3,2,1,0:T(4,128)}, f32[4,4,3,288]{3,2,1,0:T(4,128)S(1)}, u32[]{:S(2)}) copy-start(f32[4,4,3,288]{3,2,1,0:T(4,128)S(1)} %get-tuple-element.187) | copy-start | bytes 165892
  258.1 3.9 copy-start.5
  266.5 6.2 %slice-start.2 = ((s8[4718592]{0:T(1024)(128)(4,1)}), s8[4194304]{0:T(1024)(128)(4,1)S(1)}, s32[]{:S(2)}) async-start(s8[4718592]{0:T(1024)(128)(4,1)} %bitcast.219), calls=%async_computation.2 | async-start | bytes 8388608
  266.5 6.2 %slice-start.3 = ((s8[4718592]{0:T(1024)(128)(4,1)}), s8[524288]{0:T(1024)(128)(4,1)S(1)}, s32[]{:S(2)}) async-start(s8[4718592]{0:T(1024)(128)(4,1)} %bitcast.219), calls=%async_computation.3 | async-start | bytes 1048576
  272.1 14.6 %copy-start.3 = (f32[1152,768]{1,0:T(8,128)}, f32[1152,768]{1,0:T(8,128)S(1)}, u32[]{:S(2)}) copy-start(f32[1152,768]{1,0:T(8,128)S(1)} %get-tuple-element.190) | copy-start | bytes 10616836
  272.1 14.6 %slice-start.6 = ((s8[4718592]{0:T(1024)(128)(4,1)}), s8[4194304]{0:T(1024)(128)(4,1)S(1)}, s32[]{:S(2)}) async-start(s8[4718592]{0:T(1024)(128)(4,1)} %bitcast.226), calls=%async_computation.6 | async-start | bytes 8388608
  272.7 14.0 %copy-start.33 = (f32[1152]{0:T(1024)}, f32[1152]{0:T(1024)S(1)}, u32[]{:S(2)}) copy-start(f32[1152]{0:T(1024)S(1)} %add_rsqrt_fusion.1) | copy-start | bytes 13828
  272.8 13.9 %slice-start.7 = ((s8[4718592]{0:T(1024)(128)(4,1)}), s8[524288]{0:T(1024)(128)(4,1)S(1)}, s32[]{:S(2)}) async-start(s8[4718592]{0:T(1024)(128)(4,1)} %bitcast.226), calls=%async_computation.7 | async-start | bytes 1048576
  272.8 13.9 %copy-start.57 = (f32[768]{0:T(1024)S(1)}, f32[768]{0:T(1024)}, u32[]{:S(2)}) copy-start(f32[768]{0:T(1024)} %get-tuple-element.138) | copy-start | bytes 9220
  296.0 4.9 copy-start.30
  302.9 4.5 copy-start.44
  302.9 20.8 %slice-start.4 = ((s8[4718592]{0:T(1024)(128)(4,1)}), s8[4194304]{0:T(1024)(128)(4,1)S(1)}, s32[]{:S(2)}) async-start(s8[4718592]{0:T(1024)(128)(4,1)} %bitcast.222), calls=%async_computation.4 | async-start | bytes 8388608
  307.4 16.3 %copy-start.13 = (f32[1152,768]{1,0:T(8,128)}, f32[1152,768]{1,0:T(8,128)S(1)}, u32[]{:S(2)}) copy-start(f32[1152,768]{1,0:T(8,128)S(1)} %get-tuple-element.167) | copy-start | bytes 10616836
  307.4 16.3 %copy-start.4 = (f32[1152,768]{1,0:T(8,128)S(1)}, f32[1152,768]{1,0:T(8,128)}, u32[]{:S(2)}) copy-start(f32[1152,768]{1,0:T(8,128)} %copy-done.3) | copy-start | bytes 10616836
  307.4 16.3 %slice-start.5 = ((s8[4718592]{0:T(1024)(128)(4,1)}), s8[524288]{0:T(1024)(128)(4,1)S(1)}, s32[]{:S(2)}) async-start(s8[4718592]{0:T(1024)(128)(4,1)} %bitcast.222), calls=%async_computation.5 | async-start | bytes 1048576
  307.4 16.3 %copy-start.34 = (f32[1152]{0:T(1024)S(1)}, f32[1152]{0:T(1024)}, u32[]{:S(2)}) copy-start(f32[1152]{0:T(1024)} %copy-done.33) | copy-start | bytes 13828
  307.4 16.3 %copy-start.39 = (f32[768]{0:T(1024)S(1)}, f32[768]{0:T(1024)}, u32[]{:S(2)}) copy-start(f32[768]{0:T(1024)} %copy-done.38) | copy-start | bytes 9220
  348.8 10.0 %copy-start.10 = (bf16[4,4,288,1,3,64]{2,1,5,4,3,0:T(4,128)(2,1)S(1)}, bf16[4,4,288,1,3,64]{2,1,5,4,3,0:T(4,128)(2,1)}, u32[]{:S(2)}) copy-start(bf16[4,4,288,1,3,64]{2,1,5,4,3,0:T(4,128)(2,1)} %copy-done.9) | copy-start | bytes 5308420
  348.8 10.0 %copy-start.11 = (bf16[4,4,288,3,64]{2,1,4,3,0:T(4,128)(2,1)S(1)}, bf16[4,4,288,3,64]{2,1,4,3,0:T(4,128)(2,1)}, u32[]{:S(2)}) copy-start(bf16[4,4,288,3,64]{2,1,4,3,0:T(4,128)(2,1)} %reshape.195) | copy-start | bytes 5308420
  399.9 10.0 %copy-start.7 = (bf16[4,4,288,1,3,64]{2,1,5,4,3,0:T(4,128)(2,1)S(1)}, bf16[4,4,288,1,3,64]{2,1,5,4,3,0:T(4,128)(2,1)}, u32[]{:S(2)}) copy-start(bf16[4,4,288,1,3,64]{2,1,5,4,3,0:T(4,128)(2,1)} %copy-done.6) | copy-start | bytes 5308420
  409.9 6.5 %copy-start.16 = (bf16[4,4,288,1,3,64]{2,5,4,1,0,3:T(8,128)(2,1)S(1)}, bf16[4,4,288,1,3,64]{2,5,4,1,0,3:T(8,128)(2,1)}, u32[]{:S(2)}) copy-start(bf16[4,4,288,1,3,64]{2,5,4,1,0,3:T(8,128)(2,1)} %fusion.55) | copy-start | bytes 5308420
  409.9 6.5 %copy-start.17 = (bf16[4,4,288,1,3,64]{2,5,4,1,0,3:T(8,128)(2,1)S(1)}, bf16[4,4,288,1,3,64]{2,5,4,1,0,3:T(8,128)(2,1)}, u32[]{:S(2)}) copy-start(bf16[4,4,288,1,3,64]{2,5,4,1,0,3:T(8,128)(2,1)} %multiply_bitcast_fusion) | copy-start | bytes 5308420
  458.7 11.2 %copy-start.40 = (f32[768]{0:T(1024)S(1)}, f32[768]{0:T(1024)}, u32[]{:S(2)}) copy-start(f32[768]{0:T(1024)} %copy-done.38) | copy-start | bytes 9220
  458.7 11.2 %copy-start.56 = (f32[768]{0:T(1024)S(1)}, f32[768]{0:T(1024)}, u32[]{:S(2)}) copy-start(f32[768]{0:T(1024)} %copy-done.55) | copy-start | bytes 9220
  458.7 24.3 %slice-start = ((s8[5308416]{0:T(1024)(128)(4,1)}), s8[4194304]{0:T(1024)(128)(4,1)S(1)}, s32[]{:S(2)}) async-start(s8[5308416]{0:T(1024)(128)(4,1)} %bitcast.213), calls=%async_computation | async-start | bytes 8388608
  469.9 11.4 %copy-start.15 = (f32[1152,768]{1,0:T(8,128)S(1)}, f32[1152,768]{1,0:T(8,128)}, u32[]{:S(2)}) copy-start(f32[1152,768]{1,0:T(8,128)} %copy-done.14) | copy-start | bytes 10616836
  469.9 11.4 %copy-start.18 = (bf16[4,1152,192]{1,2,0:T(8,128)(2,1)S(1)}, bf16[4,1152,192]{1,2,0:T(8,128)(2,1)}, u32[]{:S(2)}) copy-start(bf16[4,1152,192]{1,2,0:T(8,128)(2,1)} %reshape.193) | copy-start | bytes 5308420
  469.9 13.1 %slice-start.1 = ((s8[5308416]{0:T(1024)(128)(4,1)}), s8[1114112]{0:T(1024)(128)(4,1)S(1)}, s32[]{:S(2)}) async-start(s8[5308416]{0:T(1024)(128)(4,1)} %bitcast.213), calls=%async_computation.1 | async-start | bytes 2228224
  497.4 10.7 %copy-start.54 = (f32[768]{0:T(1024)S(1)}, f32[768]{0:T(1024)}, u32[]{:S(2)}) copy-start(f32[768]{0:T(1024)} %get-tuple-element.128) | copy-start | bytes 9220
  497.4 10.7 %copy-start.53 = (f32[768]{0:T(1024)S(1)}, f32[768]{0:T(1024)}, u32[]{:S(2)}) copy-start(f32[768]{0:T(1024)} %get-tuple-element.133) | copy-start | bytes 9220
  497.4 10.7 %copy-start.37 = (f32[768]{0:T(1024)S(1)}, f32[768]{0:T(1024)}, u32[]{:S(2)}) copy-start(f32[768]{0:T(1024)} %get-tuple-element.168) | copy-start | bytes 9220
  497.4 10.7 %copy-start.41 = (f32[768]{0:T(1024)S(1)}, f32[768]{0:T(1024)}, u32[]{:S(2)}) copy-start(f32[768]{0:T(1024)} %get-tuple-element.130) | copy-start | bytes 9220
  497.4 10.8 %copy-start.35 = (f32[768]{0:T(1024)S(1)}, f32[768]{0:T(1024)}, u32[]{:S(2)}) copy-start(f32[768]{0:T(1024)} %get-tuple-element.134) | copy-start | bytes 9220
  497.5 10.8 %copy-start.36 = (f32[768]{0:T(1024)S(1)}, f32[768]{0:T(1024)}, u32[]{:S(2)}) copy-start(f32[768]{0:T(1024)} %get-tuple-element.166) | copy-start | bytes 9220
  497.5 10.8 %copy-start.29 = (f32[4,3,3,64]{3,2,0,1:T(4,128)S(1)}, f32[4,3,3,64]{3,2,0,1:T(4,128)}, u32[]{:S(2)}) copy-start(f32[4,3,3,64]{3,2,0,1:T(4,128)} %get-tuple-element.164) | copy-start | bytes 27652
  497.5 11.1 %copy-start.42 = (f32[4,768]{1,0:T(4,128)S(1)}, f32[4,768]{1,0:T(4,128)}, u32[]{:S(2)}) copy-start(f32[4,768]{1,0:T(4,128)} %get-tuple-element.196) | copy-start | bytes 36868
  509.8 86.2 %copy-start.25 = (f32[3,96,192]{2,1,0:T(8,128)S(1)}, f32[3,96,192]{2,1,0:T(8,128)}, u32[]{:S(2)}) copy-start(f32[3,96,192]{2,1,0:T(8,128)} %param.43) | copy-start | bytes 663556
  509.8 86.3 %copy-start.26 = (f32[3,96,192]{2,1,0:T(8,128)S(1)}, f32[3,96,192]{2,1,0:T(8,128)}, u32[]{:S(2)}) copy-start(f32[3,96,192]{2,1,0:T(8,128)} %param.42) | copy-start | bytes 663556
  509.8 86.5 %copy-start.19 = (f32[3,96,192]{1,2,0:T(8,128)S(1)}, f32[3,96,192]{1,2,0:T(8,128)}, u32[]{:S(2)}) copy-start(f32[3,96,192]{1,2,0:T(8,128)} %copy.179) | copy-start | bytes 663556
  594.7 5.3 copy-start.32
  594.7 5.4 copy-start.58
  594.7 8.5 %copy-start.28 = (f32[192,96]{1,0:T(8,128)S(1)}, f32[192,96]{1,0:T(8,128)}, u32[]{:S(2)}) copy-start(f32[192,96]{1,0:T(8,128)} %param.47) | copy-start | bytes 221188
  594.8 10.6 %copy-start.20 = (f32[3,96,768]{2,1,0:T(8,128)S(1)}, f32[3,96,768]{2,1,0:T(8,128)}, u32[]{:S(2)}) copy-start(f32[3,96,768]{2,1,0:T(8,128)} %get-tuple-element.36) | copy-start | bytes 2654212
  596.1 12.3 %copy-start.21 = (f32[96,768]{1,0:T(8,128)S(1)}, f32[96,768]{1,0:T(8,128)}, u32[]{:S(2)}) copy-start(f32[96,768]{1,0:T(8,128)} %param.50) | copy-start | bytes 884740
  596.6 14.4 %copy-start.46 = (f32[12,8]{0,1:T(8,128)S(1)}, f32[12,8]{0,1:T(8,128)}, u32[]{:S(2)}) copy-start(f32[12,8]{0,1:T(8,128)} %param.53) | copy-start | bytes 1156
  596.6 14.4 %copy-start.47 = (f32[12,8]{0,1:T(8,128)S(1)}, f32[12,8]{0,1:T(8,128)}, u32[]{:S(2)}) copy-start(f32[12,8]{0,1:T(8,128)} %param.54) | copy-start | bytes 1156
  596.6 14.4 %copy-start.48 = (f32[12,8]{0,1:T(8,128)S(1)}, f32[12,8]{0,1:T(8,128)}, u32[]{:S(2)}) copy-start(f32[12,8]{0,1:T(8,128)} %param.55) | copy-start | bytes 1156
  596.6 15.0 %copy-start.22 = (f32[768,96]{0,1:T(8,128)S(1)}, f32[768,96]{0,1:T(8,128)}, u32[]{:S(2)}) copy-start(f32[768,96]{0,1:T(8,128)} %param.56) | copy-start | bytes 884740
  596.6 15.0 %copy-start.23 = (f32[768,96]{0,1:T(8,128)S(1)}, f32[768,96]{0,1:T(8,128)}, u32[]{:S(2)}) copy-start(f32[768,96]{0,1:T(8,128)} %param.57) | copy-start | bytes 884740
  596.6 15.0 %copy-start.24 = (f32[768,96]{0,1:T(8,128)S(1)}, f32[768,96]{0,1:T(8,128)}, u32[]{:S(2)}) copy-start(f32[768,96]{0,1:T(8,128)} %param.58) | copy-start | bytes 884740
  599.2 14.3 %copy-start.1 = (s32[16,288]{1,0:T(8,128)S(1)}, s32[16,288]{1,0:T(8,128)}, u32[]{:S(2)}) copy-start(s32[16,288]{1,0:T(8,128)} %param.33) | copy-start | bytes 55300
  599.2 13.5 %copy-start.49 = (f32[6,24]{1,0:T(8,128)S(1)}, f32[6,24]{1,0:T(8,128)}, u32[]{:S(2)}) copy-start(f32[6,24]{1,0:T(8,128)} %param.59) | copy-start | bytes 1732
  599.3 13.5 %copy-start.50 = (f32[6,24]{1,0:T(8,128)S(1)}, f32[6,24]{1,0:T(8,128)}, u32[]{:S(2)}) copy-start(f32[6,24]{1,0:T(8,128)} %param.60) | copy-start | bytes 1732
  599.3 13.5 %copy-start.51 = (f32[6,24]{1,0:T(8,128)S(1)}, f32[6,24]{1,0:T(8,128)}, u32[]{:S(2)}) copy-start(f32[6,24]{1,0:T(8,128)} %param.61) | copy-start | bytes 1732
  (5 other events, 8.6 us)
